TPU v7x, 32 devices: a whole 2x2x4 slice. The times are simulated.
32 devices in a mesh: tok: 2 (over core), feat: 16 (over z, y, x).
Axes of the slice: x: 2, y: 2, z: 4, core: 2. Of those that a mesh axis runs over, the one named last changes fastest.
Arguments:
- inputs: bfloat16 [8192, 8192], P('feat', 'tok'), may hold values from -6 to 6
- first_weight: bfloat16 [64, 128, 128], P('feat'), may hold values from -0.5 to 0.5
- second_weight: bfloat16 [64, 128, 512], P('feat'), may hold values from -0.5 to 0.5
- third_weight: bfloat16 [64, 512, 128], P('feat'), may hold values from -0.25 to 0.25
- fourth_weight: bfloat16 [64, 128, 128], P('feat'), may hold values from -0.5 to 0.5
- output_grad: bfloat16 [8192, 8192], P(None, ('tok', 'feat')), may hold values from -6 to 6
Outputs:
- layer_out: bfloat16 [8192, 8192], P(None, ('tok', 'feat'))
- input_grad: bfloat16 [8192, 8192], P('feat', 'tok')
- first_grad: float32 [64, 128, 128], P('feat')
- second_grad: float32 [64, 128, 512], P('feat')
- third_grad: float32 [64, 512, 128], P('feat')
- fourth_grad: float32 [64, 128, 128], P('feat')
All inputs are finite; a program needn't handle non-finite values.
Results may differ from a plain program's by a relative error of at most 0.0074.
Values may be sent and summed in bfloat16 or wider, within the bound.
No kernel may reach another device: no remote copies, remote signals or barrier semaphores. Data moves between devices by JAX's collectives and lax.ppermute only.
A program may use at most 192 MiB of HBM per device.

v0:
```python
import functools

import jax
import jax.numpy as jnp
from jax import lax
from jax.experimental import pallas as pl
from jax.experimental.pallas import tpu as pltpu
from jax.sharding import PartitionSpec as P

BF = jnp.bfloat16
F32 = jnp.float32
CB = 4
TT = 256
STEP = 4
PAIR = 2


def gelu_tanh(value):
    return jax.nn.gelu(value, approximate=True)


def into_raw(source, weight, parts):
    count, in_width, out_width = weight.shape
    shaped = weight.reshape(count, in_width, out_width // (parts * count), parts, count)
    return jnp.einsum("cit,cikdq->dckqt", source, shaped, preferred_element_type=F32)


def from_blocks(grad, weight, parts):
    count, in_width, out_width = weight.shape
    shaped = weight.reshape(count, in_width // (parts * count), parts, count, out_width)
    return jnp.einsum("qot,qksco->sckqt", grad, shaped, preferred_element_type=F32)


def raw_to_blocks(received):
    count = received.shape[1]
    tokens = received.shape[4]
    width = received.shape[0] * count * received.shape[2]
    return jnp.transpose(received, (3, 2, 0, 1, 4)).reshape(count, width, tokens)


def raw_back(received, weight, parts):
    count, in_width, out_width = weight.shape
    shaped = weight.reshape(count, in_width, out_width // (parts * count), parts, count)
    return jnp.einsum("dckqt,cikdq->cit", received, shaped, preferred_element_type=F32)


def raw_outer(source, received):
    count, in_width, _ = source.shape
    out_width = received.shape[0] * received.shape[2] * received.shape[3]
    grad = jnp.einsum("cit,dckqt->cikdq", source, received, preferred_element_type=F32)
    return grad.reshape(count, in_width, out_width)


def local_any(inputs, first_weight, second_weight, third_weight, fourth_weight, output_grad):
    count, width, _ = first_weight.shape
    parts = lax.axis_size("feat")
    blocks_all = count * parts
    tok_dev = inputs.shape[1]
    tok_part = output_grad.shape[1]
    scale = (tok_dev * lax.axis_size("tok")) ** (-0.5)
    source = inputs.reshape(count, width, tok_dev)
    first_raw = into_raw(source, first_weight, parts).astype(BF)
    first_perm = raw_to_blocks(
        lax.all_to_all(first_raw, "feat", split_axis=0, concat_axis=0, tiled=True)
    )
    pre = jnp.einsum("qit,qio->qot", first_perm, second_weight, preferred_element_type=F32).astype(BF)
    act = gelu_tanh(pre.astype(F32)).astype(BF)
    third_raw = into_raw(act, third_weight, parts).astype(BF)
    permuted = raw_to_blocks(
        lax.all_to_all(third_raw, "feat", split_axis=0, concat_axis=0, tiled=True)
    )
    result = jnp.einsum("qit,qio->qot", permuted, fourth_weight, preferred_element_type=F32).astype(BF)
    out_tokens = lax.all_to_all(result, "feat", split_axis=2, concat_axis=0, tiled=True)
    layer_out = out_tokens.reshape(blocks_all * width, tok_part)
    grad_blocks = lax.all_to_all(
        output_grad.reshape(blocks_all, width, tok_part), "feat", split_axis=0, concat_axis=2, tiled=True
    )
    fourth_sum = jnp.einsum("qit,qot->qio", permuted, grad_blocks, preferred_element_type=F32)
    back_raw = from_blocks(grad_blocks, fourth_weight, parts).astype(BF)
    third_back = lax.all_to_all(back_raw, "feat", split_axis=0, concat_axis=0, tiled=True)
    hidden_grad = raw_back(third_back, third_weight, parts)
    third_sum = raw_outer(act, third_back)
    pre_grad = jax.vjp(gelu_tanh, pre.astype(F32))[1](hidden_grad)[0].astype(BF)
    second_sum = jnp.einsum("qit,qot->qio", first_perm, pre_grad, preferred_element_type=F32)
    first_raw_back = from_blocks(pre_grad, second_weight, parts).astype(BF)
    first_back = lax.all_to_all(first_raw_back, "feat", split_axis=0, concat_axis=0, tiled=True)
    first_sum = raw_outer(source, first_back)
    input_grad = raw_back(first_back, first_weight, parts).astype(BF).reshape(count * width, tok_dev)
    totals = lax.psum((first_sum, second_sum, third_sum, fourth_sum), "tok")
    return (layer_out, input_grad) + tuple(total * scale for total in totals)


def rows8(parts):
    return jnp.concatenate([part.astype(F32) for part in parts], axis=0)


def masked(compact):
    rows, width = compact.shape
    wide = compact.astype(F32)
    row = lax.broadcasted_iota(jnp.int32, (rows, width), 0) % CB
    return jnp.concatenate([jnp.where(row == c, wide, 0.0) for c in range(CB)], axis=1)


def compacted(wide):
    rows, width = wide.shape[0], wide.shape[1] // CB
    row = lax.broadcasted_iota(jnp.int32, (rows, width), 0) % CB
    kept = wide[:, :width]
    for c in range(1, CB):
        kept = jnp.where(row == c, wide[:, c * width : (c + 1) * width], kept)
    return kept


def dot(a, b, a_dim=1, b_dim=0):
    return lax.dot_general(a, b, (((a_dim,), (b_dim,)), ((), ())), preferred_element_type=F32)


def split_kernel(grouping, who, x0, x1, a_ref, *rest):
    outs, big = rest[:8], rest[8]
    f = who[0]

    @pl.when(pl.program_id(0) == 0)
    def _():
        big[...] = masked(jnp.concatenate([a_ref[f ^ r] for r in range(16)], axis=0)).astype(BF)

    for e, x in enumerate((x0, x1)):
        for n in range(PAIR):
            y = dot(big[...], x[:, TT * n : TT * n + TT])
            for r in range(16):
                h, s = e ^ (r >> 3), 8 * e + (r & 7)
                i, j = (s >> 2, s & 3) if grouping[h] == "z" else (s & 3, s >> 2)
                outs[4 * h + i][j, :, n] = y[32 * r : 32 * r + 32].reshape(4, 8, TT).astype(BF)


def gathered(who, a_ref, n):
    f, tok = who[0], who[1]
    rows = [a_ref[((f ^ r) >> 3) ^ tok, n, (f ^ r) & 7] for r in range(16)]
    return masked(jnp.concatenate(rows, axis=0)).astype(BF)


def group_rows(at):
    return pl.ds(pl.multiple_of(512 * at, 512), 512)


def back_kernel(who, og, a_ref, *outs):
    for n in range(STEP):
        at = (who[0] & (STEP - 1)) ^ n
        y = dot(gathered(who, a_ref, n), og[group_rows(at), :])
        for r in range(16):
            outs[r >> 3][(who[0] & 7) ^ (r & 7), at] = y[32 * r : 32 * r + 32].reshape(4, 8, TT).astype(BF)


def middle_kernel(grouping, who, *refs):
    x_near, x_far, tb, w_ref = refs[:4], refs[4:7], refs[7], refs[8]
    fb_out, ta_out, g_ref = refs[9:13], refs[13], refs[14]
    sg, tg = refs[15], refs[16]
    f = who[0]

    def place(s):
        return (s >> 2, s & 3) if grouping == "z" else (s & 3, s >> 2)

    w2f = rows8([w_ref[0, 0, f ^ s] for s in range(16)])
    w2 = w2f.astype(BF)
    w2t = w2f.T.astype(BF)
    w3tf = w_ref[0, 1].astype(F32).reshape(128, w2.shape[1])
    w3t = w3tf.astype(BF)
    w3 = w3tf.T.astype(BF)
    for q in range(8):
        at = (f & 7) ^ q
        pieces = []
        for s in range(16):
            i, j = place(s)
            pieces.append(x_near[i][0, 0, at] if j == 0 else x_far[j - 1][i, 0, at])
        x = rows8(pieces).astype(BF)
        back = tb[at, :, 0].astype(F32).reshape(128, TT).astype(BF)
        v = dot(w2t, x).astype(BF).astype(F32)
        hidden_grad = dot(w3, back)
        vv = v * v
        t = jnp.tanh(v * (0.7978845608028654 + (0.7978845608028654 * 0.044715) * vv))
        half = 0.5 + 0.5 * t
        hidden = (v * half).astype(BF)
        slope = half + (0.5 * v) * (1.0 - t * t) * (
            0.7978845608028654 + (3 * 0.7978845608028654 * 0.044715) * vv
        )
        pre_grad = (hidden_grad * slope).astype(BF)
        ta_out[at, :, 0] = dot(w3t, hidden).reshape(16, 8, TT).astype(BF)
        fb = dot(w2, pre_grad)
        for s in range(16):
            i, j = place(s)
            fb_out[i][j, 0, at] = fb[8 * s : 8 * s + 8].astype(BF)
        s_now = dot(x, pre_grad, 1, 1)
        t_now = dot(back, hidden, 1, 1)
        if q == 0:
            sg[...] = s_now
            tg[...] = t_now
        else:
            sg[...] += s_now
            tg[...] += t_now
    total = sg[...]
    for s in range(16):
        g_ref[0, 0, f ^ s] = total[8 * s : 8 * s + 8]
    g_ref[0, 1] = tg[...].reshape(16, 8, -1)


def token_kernel(who, *refs):
    pieces, og, a_ref, out, g_ref = refs[:2], refs[2], refs[3], refs[4], refs[5]
    f, tok = who[0], who[1]
    for n in range(STEP):
        at = (f & (STEP - 1)) ^ n
        parts = [pieces[r >> 3][(f & 7) ^ (r & 7), at] for r in range(16)]
        rows = jnp.concatenate([part.astype(F32).reshape(32, TT) for part in parts], axis=0).astype(BF)
        out[group_rows(at), :] = dot(gathered(who, a_ref, n), rows, 0, 0).astype(BF)
        g = compacted(dot(rows, og[group_rows(at), :], 1, 1))
        for r in range(16):
            g_ref[((f ^ r) >> 3) ^ tok, n, (f ^ r) & 7] = g[32 * r : 32 * r + 32]


def finish_kernel(grouping, who, *refs):
    chunks = (refs[:7], refs[7:14])
    x, a_ref, out, g_ref, big, acc = refs[14:20]
    f = who[0]
    e = pl.program_id(0)
    t = pl.program_id(1)

    @pl.when((e == 0) & (t == 0))
    def _():
        big[...] = masked(jnp.concatenate([a_ref[f ^ r] for r in range(16)], axis=0)).T.astype(BF)
        acc[...] = jnp.zeros_like(acc)

    def piece(h, s, n):
        i, j = (s >> 2, s & 3) if grouping[h] == "z" else (s & 3, s >> 2)
        got = chunks[h][i][0, :, n] if j == 0 else chunks[h][3 + j][i, :, n]
        return got.astype(F32).reshape(32, TT)

    def run(half):
        rows = jnp.concatenate(
            [
                jnp.concatenate([piece(half ^ (r >> 3), 8 * half + (r & 7), n) for n in range(PAIR)], axis=1)
                for r in range(16)
            ],
            axis=0,
        ).astype(BF)
        out[...] = dot(big[...], rows).astype(BF)
        acc[...] += dot(rows, x[...], 1, 1)

    @pl.when(e == 0)
    def _():
        run(0)

    @pl.when(e == 1)
    def _():
        run(1)

    @pl.when((e == 1) & (t == pl.num_programs(1) - 1))
    def _():
        g = compacted(acc[...])
        for r in range(16):
            g_ref[f ^ r] = g[32 * r : 32 * r + 32]


def call(kernel, grid, in_specs, out_specs, out_shape, scratch=(), flops=0, bytes_=0):
    return pl.pallas_call(
        kernel,
        grid_spec=pltpu.PrefetchScalarGridSpec(
            num_scalar_prefetch=1, grid=grid, in_specs=in_specs, out_specs=out_specs, scratch_shapes=list(scratch)
        ),
        out_shape=out_shape,
        compiler_params=pltpu.CompilerParams(
            dimension_semantics=("arbitrary",) * len(grid), vmem_limit_bytes=56 * 2**20
        ),
        cost_estimate=pl.CostEstimate(flops=flops, transcendentals=0, bytes_accessed=bytes_),
    )


def shape(dims, dtype=BF):
    return jax.ShapeDtypeStruct(dims, dtype)


def flip(value, bits):
    return lax.ppermute(value, "feat", [(i, i ^ bits) for i in range(16)])


def spread(value):
    groups = [list(range(8)), list(range(8, 16))]
    return lax.all_to_all(value, "feat", 0, 0, axis_index_groups=groups, tiled=True)


def swap(value):
    return lax.ppermute(value, "tok", [(0, 1), (1, 0)])


def two_stage(groups, first):
    one, two = (4, 1) if first == "z" else (1, 4)
    near = [groups[0]] + [flip(groups[i], one * i) for i in (1, 2, 3)]
    far = [flip(jnp.stack([n[j] for n in near]), two * j) for j in (1, 2, 3)]
    return near + far


def local_halves(inputs, first_weight, second_weight, third_weight, fourth_weight, output_grad):
    _, width, hidden = second_weight.shape
    tok_dev, tok_part = inputs.shape[1], output_grad.shape[1]
    scale = (tok_dev * 2) ** (-0.5)
    tiles = tok_dev // 2 // TT
    steps = tiles // PAIR
    f, tok = lax.axis_index("feat"), lax.axis_index("tok")
    who = jnp.stack([f, tok, f >> 3]).astype(jnp.int32)
    grouping = ("xy", "z")
    order = (1, 0)

    a_one = first_weight.reshape(CB, width, 2, 64).transpose(3, 2, 0, 1).reshape(16, 32, width)
    a_four = fourth_weight.reshape(CB, 2, 64, width).transpose(2, 1, 0, 3).reshape(2, 8, 32, width)
    w_two = second_weight.reshape(CB, 2, 16, CB, hidden).transpose(0, 2, 1, 3, 4).reshape(CB, 16, 8, hidden)
    w_three = third_weight.reshape(CB, hidden, 2, 16, CB).transpose(0, 3, 2, 4, 1).reshape(CB, 16, 8, hidden)
    w_own = jnp.stack([w_two, w_three], axis=1)

    got = lax.dynamic_slice_in_dim(a_four, tok, 1, 0)
    got = jnp.concatenate([got] + [flip(got, bits) for bits in (4, 8, 12)], axis=0)
    got = [got] + [flip(got, bits) for bits in (1, 2, 3)]
    got = jnp.stack(got, axis=1).reshape(16, 8, 32, width)
    a_all = jnp.stack([got, swap(got)])

    w_half = flip(lax.dynamic_slice_in_dim(w_own, 2 * tok, 2, 0), 8)
    w_far = jnp.concatenate([w_half, swap(w_half)], axis=0)

    tile_specs = [pl.BlockSpec((512, PAIR * TT), lambda t, w, e=e: (0, (w[2] ^ e) * steps + t)) for e in (0, 1)]
    whole_a = pl.BlockSpec((16, 32, width), lambda t, w: (0, 0, 0))
    group = shape((4, 4, tiles, 8, TT))
    sent = call(
        functools.partial(split_kernel, grouping), (steps,),
        tile_specs + [whole_a],
        [pl.BlockSpec((4, 4, PAIR, 8, TT), lambda t, w: (0, 0, t, 0, 0))] * 8,
        [group] * 8,
        [pltpu.VMEM((512, 512), BF)],
        2 * 512 * 512 * tok_dev, 4 * 512 * tok_dev,
    )(who, inputs, inputs, a_one)
    arrived = {h: two_stage(sent[4 * h : 4 * h + 4], grouping[h]) for h in order}

    a_spec = pl.BlockSpec((2, STEP, 8, 32, width), lambda n, w: (0, n, 0, 0, 0))
    og_spec = pl.BlockSpec((512 * STEP, TT), lambda n, w: ((w[0] // STEP) ^ n, 0))
    back = call(
        back_kernel, (16 // STEP,), [og_spec, a_spec],
        [pl.BlockSpec((8, STEP, 4, 8, TT), lambda n, w: (0, (w[0] // STEP) ^ n, 0, 0, 0))] * 2,
        [shape((8, 16, 4, 8, TT))] * 2, (), 2 * 512 * 8192 * TT, 4 * 8192 * TT,
    )(who, output_grad, a_all)
    back = {h: spread(back[h]) for h in order}

    results = {}
    near_spec = pl.BlockSpec((1, 1, tiles, 8, TT), lambda l, w: (0, l, 0, 0, 0))
    far_spec = pl.BlockSpec((4, 1, tiles, 8, TT), lambda l, w: (0, l, 0, 0, 0))
    rows_spec = pl.BlockSpec((8, 16, 1, 8, TT), lambda l, w: (0, 0, l, 0, 0))
    for h in order:
        w_spec = pl.BlockSpec((1, 2, 16, 8, hidden), lambda l, w, h=h: (l ^ (2 * w[1] * h), 0, 0, 0, 0))
        g_spec = pl.BlockSpec((1, 2, 16, 8, hidden), lambda l, w: (l ^ (2 * w[1]), 0, 0, 0, 0))
        results[h] = call(
            functools.partial(middle_kernel, grouping[h]), (4,),
            [near_spec] * 4 + [far_spec] * 3 + [rows_spec, w_spec],
            [far_spec] * 4 + [rows_spec, g_spec],
            [group] * 4 + [shape((8, 16, 4, 8, TT))] + [shape((4, 2, 16, 8, hidden), F32)],
            [pltpu.VMEM((128, hidden), F32)] * 2,
            12 * 4 * 128 * hidden * tok_dev // 2, 20 * 2**20,
        )(who, *arrived[h], back[h], w_far if h else w_own)
    returned = {h: two_stage(results[h][:4], grouping[h]) for h in order}
    acts = {h: spread(results[h][4]) for h in order}

    near_spec = pl.BlockSpec((1, 4, PAIR, 8, TT), lambda e, t, w: (0, 0, t, 0, 0))
    far_spec = pl.BlockSpec((4, 4, PAIR, 8, TT), lambda e, t, w: (0, 0, t, 0, 0))
    tile_spec = pl.BlockSpec((512, PAIR * TT), lambda e, t, w: (0, (w[2] ^ e) * steps + t))
    whole_a = pl.BlockSpec((16, 32, width), lambda e, t, w: (0, 0, 0))
    input_grad, first = call(
        functools.partial(finish_kernel, grouping), (2, steps),
        ([near_spec] * 4 + [far_spec] * 3) * 2 + [tile_spec, whole_a],
        [tile_spec, whole_a],
        [shape((512, tok_dev)), shape((16, 32, width), F32)],
        [pltpu.VMEM((512, 512), BF), pltpu.VMEM((512, 512), F32)],
        4 * 512 * 512 * tok_dev, 6 * 512 * tok_dev,
    )(who, *returned[0], *returned[1], inputs, a_one)

    layer_out, fourth = call(
        token_kernel, (16 // STEP,),
        [pl.BlockSpec((8, STEP, 4, 8, TT), lambda n, w: (0, (w[0] // STEP) ^ n, 0, 0, 0))] * 2 + [og_spec, a_spec],
        [og_spec, a_spec],
        [shape((8192, tok_part)), shape((2, 16, 8, 32, width), F32)], (),
        4 * 512 * 8192 * TT, 6 * 8192 * TT,
    )(who, acts[0], acts[1], output_grad, a_all)

    def both(mine):
        other = swap(mine)
        low, high = jnp.where(tok == 0, mine, other), jnp.where(tok == 0, other, mine)
        return jnp.concatenate([low, high], axis=0)

    kept = [results[h][5][:2] + swap(results[h][5][2:].astype(BF)).astype(F32) for h in (0, 1)]
    middle = both(kept[0] + flip(kept[1].astype(BF), 8).astype(F32)) * scale
    second = middle[:, 0].reshape(CB, 16, 2, CB, hidden).transpose(0, 2, 1, 3, 4).reshape(CB, width, hidden)
    third = middle[:, 1].reshape(CB, 16, 2, CB, hidden).transpose(0, 4, 2, 1, 3).reshape(CB, hidden, width)

    part = fourth[0] + swap(fourth[1].astype(BF)).astype(F32)
    part = part.reshape(4, 4, 8, 32, width)
    part = part[:, 0] + sum(flip(part[:, j].astype(BF), j).astype(F32) for j in (1, 2, 3))
    part = part[0] + sum(flip(part[j].astype(BF), 4 * j).astype(F32) for j in (1, 2, 3))
    fourth = both(part).reshape(16, CB, 2, CB, width) * scale
    fourth = fourth.transpose(3, 2, 0, 1, 4).reshape(CB, width, width)

    first = (first + swap(first)).reshape(16, CB, 2, CB, width) * scale
    first = first.transpose(3, 4, 2, 0, 1).reshape(CB, width, width)
    return (layer_out, input_grad, first, second, third, fourth)


def solution(mesh):
    placed = (
        P("feat", "tok"),
        P("feat", None, None),
        P("feat", None, None),
        P("feat", None, None),
        P("feat", None, None),
        P(None, ("tok", "feat")),
    )

    def local(inputs, first_weight, second_weight, third_weight, fourth_weight, output_grad):
        fits = (
            mesh.shape["feat"] == 16
            and mesh.shape["tok"] == 2
            and first_weight.shape == (CB, 128, 128)
            and output_grad.shape == (8192, TT)
            and inputs.shape[1] == 16 * TT
        )
        run = local_halves if fits else local_any
        return run(inputs, first_weight, second_weight, third_weight, fourth_weight, output_grad)

    return jax.shard_map(
        local,
        mesh=mesh,
        in_specs=placed,
        out_specs=(
            P(None, ("tok", "feat")),
            P("feat", "tok"),
            P("feat", None, None),
            P("feat", None, None),
            P("feat", None, None),
            P("feat", None, None),
        ),
        check_vma=False,
    )
```

profile of v0, /device:TPU:14, one launch (start us, length us, event | category | flops | bytes accessed | tf_op | source)
XLA Modules:
  0.0 517.9 jit_solution(14586969011435333105)
XLA Ops:
  5.8 3.1 collective-permute-done.8
  14.1 4.8 collective-permute-done.10
  20.2 4.1 collective-permute-done.11
  28.7 7.3 %shard_map.110 = (bf16[8,16,4,8,256]{4,3,2,1,0:T(8,128)(2,1)}, bf16[8,16,4,8,256]{4,3,2,1,0:T(8,128)(2,1)}) custom-call(s32[3]{0:T(128)} %pad_add_fusion.who, bf16[8192,256]{1,0:T(8,128)(2,1)} %refs_2_.1, bf16[2,16,8,32,128]{4,3,2,1,0:T(8,128)(2,1)} %pad_maximum_fusion.a_ref.refs_3_), custom_call_target="tpu_custom_call" | custom-call | flops 2147483648 | bytes 8388608 | tf_op jit(solution)/shard_map/pallas_call | solution.py:339
  35.9 30.0 %all_to_all.20.refs_7_ = bf16[8,16,4,8,256]{4,3,2,1,0:T(8,128)(2,1)} all-to-all(bf16[8,16,4,8,256]{4,3,2,1,0:T(8,128)(2,1)} %get-tuple-element.36), channel_id=1, replica_groups={{0,1,2,3,4,5,6,7},{8,9,10,11,12,13,14,15},{16,17,18,19,20,21,22,23},{24..., dimensions={0} | all-to-all | bytes 4194304 | tf_op jit(solution)/shard_map/all_to_all | solution.py:284
  66.0 6.6 %all-to-all-start.2 = ((bf16[8,16,4,8,256]{4,3,2,1,0:T(8,128)(2,1)}), bf16[8,16,4,8,256]{4,3,2,1,0:T(8,128)(2,1)S(1)}, u32[]{:S(2)}, u32[]{:S(2)}) async-start(bf16[8,16,4,8,256]{4,3,2,1,0:T(8,128)(2,1)} %get-tuple-element.42), calls=%async_computation.2 | async-start | bytes 4194304 | tf_op jit(solution)/shard_map/all_to_all | solution.py:284
  73.5 7.0 %shard_map.109 = (bf16[4,4,8,8,256]{4,3,2,1,0:T(8,128)(2,1)}, bf16[4,4,8,8,256]{4,3,2,1,0:T(8,128)(2,1)}, bf16[4,4,8,8,256]{4,3,2,1,0:T(8,128)(2,1)}, bf16[4,4,8...) custom-call(s32[3]{0:T(128)} %pad_add_fusion.who, ...), custom_call_target="tpu_custom_call" | custom-call | flops 2147483648 | bytes 8388608 | tf_op jit(solution)/shard_map/pallas_call | solution.py:327
  85.0 23.6 %collective-permute-done.refs_1_ = bf16[4,4,8,8,256]{4,3,2,1,0:T(8,128)(2,1)S(1)} collective-permute-done((bf16[4,4,8,8,256]{4,3,2,1,0:T(8,128)(2,1)}, bf16[4,4,8,8,256]{4,3,2,1,0:T(8,128)(2,1)S(1)}, u32[]{:S(2)}, u32[]{:S(2)}) %collective-permute-start) | collective-permute-done | bytes 524320 | tf_op jit(solution)/shard_map/ppermute | solution.py:279
  109.4 10.1 %collective-permute-done.2.refs_3_ = bf16[4,4,8,8,256]{4,3,2,1,0:T(8,128)(2,1)S(1)} collective-permute-done((bf16[4,4,8,8,256]{4,3,2,1,0:T(8,128)(2,1)}, bf16[4,4,8,8,256]{4,3,2,1,0:T(8,128)(2,1)S(1)}, u32[]{:S(2)}, u32[]{:S(2)}) %collective-permute-start.2) | collective-permute-done | bytes 524320 | tf_op jit(solution)/shard_map/ppermute | solution.py:279
  129.9 10.5 %collective-permute-done.3.refs_4_ = bf16[4,4,8,8,256]{4,3,2,1,0:T(8,128)(2,1)} collective-permute-done((bf16[4,4,8,8,256]{4,3,2,1,0:T(8,128)(2,1)}, bf16[4,4,8,8,256]{4,3,2,1,0:T(8,128)(2,1)}, u32[]{:S(2)}, u32[]{:S(2)}) %collective-permute-start.3) | collective-permute-done | bytes 524320 | tf_op jit(solution)/shard_map/ppermute | solution.py:279
  140.4 17.1 %collective-permute-done.4.refs_5_ = bf16[4,4,8,8,256]{4,3,2,1,0:T(8,128)(2,1)} collective-permute-done((bf16[4,4,8,8,256]{4,3,2,1,0:T(8,128)(2,1)}, bf16[4,4,8,8,256]{4,3,2,1,0:T(8,128)(2,1)}, u32[]{:S(2)}, u32[]{:S(2)}) %collective-permute-start.4) | collective-permute-done | bytes 524320 | tf_op jit(solution)/shard_map/ppermute | solution.py:279
  157.5 13.0 %collective-permute-done.5.refs_6_ = bf16[4,4,8,8,256]{4,3,2,1,0:T(8,128)(2,1)} collective-permute-done((bf16[4,4,8,8,256]{4,3,2,1,0:T(8,128)(2,1)}, bf16[4,4,8,8,256]{4,3,2,1,0:T(8,128)(2,1)}, u32[]{:S(2)}, u32[]{:S(2)}) %collective-permute-start.5) | collective-permute-done | bytes 524320 | tf_op jit(solution)/shard_map/ppermute | solution.py:279
  170.4 26.0 %shard_map.111 = (bf16[4,4,8,8,256]{4,3,2,1,0:T(8,128)(2,1)}, bf16[4,4,8,8,256]{4,3,2,1,0:T(8,128)(2,1)}, bf16[4,4,8,8,256]{4,3,2,1,0:T(8,128)(2,1)}, bf16[4,4,8...) custom-call(s32[3]{0:T(128)} %pad_add_fusion.who, ...), custom_call_target="tpu_custom_call" | custom-call | flops 6442450944 | bytes 20971520 | tf_op jit(solution)/shard_map/pallas_call | solution.py:353
  197.9 5.3 %all-to-all-start.1 = ((bf16[8,16,4,8,256]{4,3,2,1,0:T(8,128)(2,1)}), bf16[8,16,4,8,256]{4,3,2,1,0:T(8,128)(2,1)S(1)}, u32[]{:S(2)}, u32[]{:S(2)}) async-start(bf16[8,16,4,8,256]{4,3,2,1,0:T(8,128)(2,1)} %get-tuple-element.37), calls=%async_computation.1 | async-start | bytes 4194304 | tf_op jit(solution)/shard_map/all_to_all | solution.py:284
  203.8 3.0 collective-permute-start.19
  207.9 51.6 %collective-permute-done.13.refs_1_ = bf16[4,4,8,8,256]{4,3,2,1,0:T(8,128)(2,1)} collective-permute-done((bf16[4,4,8,8,256]{4,3,2,1,0:T(8,128)(2,1)}, bf16[4,4,8,8,256]{4,3,2,1,0:T(8,128)(2,1)}, u32[]{:S(2)}, u32[]{:S(2)}) %collective-permute-start.13) | collective-permute-done | bytes 524320 | tf_op jit(solution)/shard_map/ppermute | solution.py:279
  261.6 11.4 %collective-permute-done.15.refs_3_ = bf16[4,4,8,8,256]{4,3,2,1,0:T(8,128)(2,1)S(1)} collective-permute-done((bf16[4,4,8,8,256]{4,3,2,1,0:T(8,128)(2,1)}, bf16[4,4,8,8,256]{4,3,2,1,0:T(8,128)(2,1)S(1)}, u32[]{:S(2)}, u32[]{:S(2)}) %collective-permute-start.15) | collective-permute-done | bytes 524320 | tf_op jit(solution)/shard_map/ppermute | solution.py:279
  278.0 9.9 %collective-permute-done.16.refs_4_ = bf16[4,4,8,8,256]{4,3,2,1,0:T(8,128)(2,1)S(1)} collective-permute-done((bf16[4,4,8,8,256]{4,3,2,1,0:T(8,128)(2,1)S(1)}, bf16[4,4,8,8,256]{4,3,2,1,0:T(8,128)(2,1)S(1)}, u32[]{:S(2)}, u32[]{:S(2)}) %collective-permute-start.16) | collective-permute-done | bytes 524320 | tf_op jit(solution)/shard_map/ppermute | solution.py:279
  287.9 11.6 %collective-permute-done.17.refs_5_ = bf16[4,4,8,8,256]{4,3,2,1,0:T(8,128)(2,1)S(1)} collective-permute-done((bf16[4,4,8,8,256]{4,3,2,1,0:T(8,128)(2,1)S(1)}, bf16[4,4,8,8,256]{4,3,2,1,0:T(8,128)(2,1)S(1)}, u32[]{:S(2)}, u32[]{:S(2)}) %collective-permute-start.17) | collective-permute-done | bytes 524320 | tf_op jit(solution)/shard_map/ppermute | solution.py:279
  301.0 26.1 %shard_map.112 = (bf16[4,4,8,8,256]{4,3,2,1,0:T(8,128)(2,1)}, bf16[4,4,8,8,256]{4,3,2,1,0:T(8,128)(2,1)}, bf16[4,4,8,8,256]{4,3,2,1,0:T(8,128)(2,1)}, bf16[4,4,8...) custom-call(s32[3]{0:T(128)} %pad_add_fusion.who, ...), custom_call_target="tpu_custom_call" | custom-call | flops 6442450944 | bytes 20971520 | tf_op jit(solution)/shard_map/pallas_call | solution.py:353
  328.4 5.2 %all-to-all-start.3 = ((bf16[8,16,4,8,256]{4,3,2,1,0:T(8,128)(2,1)}), bf16[8,16,4,8,256]{4,3,2,1,0:T(8,128)(2,1)}, u32[]{:S(2)}, u32[]{:S(2)}) async-start(bf16[8,16,4,8,256]{4,3,2,1,0:T(8,128)(2,1)} %get-tuple-element.43), calls=%async_computation.3 | async-start | bytes 4194304 | tf_op jit(solution)/shard_map/all_to_all | solution.py:284
  341.8 37.3 %collective-permute-done.27.refs_8_ = bf16[4,4,8,8,256]{4,3,2,1,0:T(8,128)(2,1)S(1)} collective-permute-done((bf16[4,4,8,8,256]{4,3,2,1,0:T(8,128)(2,1)}, bf16[4,4,8,8,256]{4,3,2,1,0:T(8,128)(2,1)S(1)}, u32[]{:S(2)}, u32[]{:S(2)}) %collective-permute-start.27) | collective-permute-done | bytes 524320 | tf_op jit(solution)/shard_map/ppermute | solution.py:279
  379.7 4.6 collective-permute-done.28.refs_9_
  389.8 15.8 %collective-permute-done.22.refs_2_ = bf16[4,4,8,8,256]{4,3,2,1,0:T(8,128)(2,1)S(1)} collective-permute-done((bf16[4,4,8,8,256]{4,3,2,1,0:T(8,128)(2,1)S(1)}, bf16[4,4,8,8,256]{4,3,2,1,0:T(8,128)(2,1)S(1)}, u32[]{:S(2)}, u32[]{:S(2)}) %collective-permute-start.22) | collective-permute-done | bytes 524320 | tf_op jit(solution)/shard_map/ppermute | solution.py:279
  415.6 10.7 %shard_map.113 = (bf16[8192,256]{1,0:T(8,128)(2,1)}, f32[2,16,8,32,128]{4,3,2,1,0:T(8,128)}) custom-call(s32[3]{0:T(128)} %pad_add_fusion.who, bf16[8,16,4,8,256]{4,3,2,1,0:T(8,128)(2,1)} %copy-done, bf16[8,16,4,8,256]{4,3,2,1,0:T(8,128)(2,1)} %all-to-all-done.3.refs_1_, bf16[8192,256]{1,0:T(8,128)(2,1)} %refs_2_.1, ...), custom_call_target="tpu_custom_call" | custom-call | flops 4294967296 | bytes 12582912 | tf_op jit(solution)/shard_map/pallas_call | solution.py:377
  427.4 2.8 fusion
  430.3 25.7 %collective-permute-done.25.refs_5_ = bf16[4,4,8,8,256]{4,3,2,1,0:T(8,128)(2,1)} collective-permute-done((bf16[4,4,8,8,256]{4,3,2,1,0:T(8,128)(2,1)}, bf16[4,4,8,8,256]{4,3,2,1,0:T(8,128)(2,1)}, u32[]{:S(2)}, u32[]{:S(2)}) %collective-permute-start.25) | collective-permute-done | bytes 524320 | tf_op jit(solution)/shard_map/ppermute | solution.py:279
  456.0 14.1 %collective-permute-done.26.refs_6_ = bf16[4,4,8,8,256]{4,3,2,1,0:T(8,128)(2,1)} collective-permute-done((bf16[4,4,8,8,256]{4,3,2,1,0:T(8,128)(2,1)S(1)}, bf16[4,4,8,8,256]{4,3,2,1,0:T(8,128)(2,1)}, u32[]{:S(2)}, u32[]{:S(2)}) %collective-permute-start.26) | collective-permute-done | bytes 524320 | tf_op jit(solution)/shard_map/ppermute | solution.py:279
  470.1 12.4 %shard_map.114 = (bf16[512,4096]{1,0:T(8,128)(2,1)}, f32[16,32,128]{2,1,0:T(8,128)}) custom-call(s32[3]{0:T(128)} %pad_add_fusion.who, bf16[4,4,8,8,256]{4,3,2,1,0:T(8,128)(2,1)} %get-tuple-element.45.refs_0_, bf16[4,4,8,8,256]{4,3,2,1,0:T(8,128)(2,1)} %copy-done.11, bf16[4,4,8,8,256]{4,3,2,1,0:T(8,128)(2,1)} %copy-done.12, ...), custom_call_target="tpu_custom_call" | custom-call | flops 4294967296 | bytes 12582912 | tf_op jit(solution)/shard_map/pallas_call | solution.py:368
  492.6 5.5 %collective-permute-done.39 = bf16[4,8,32,128]{3,2,1,0:T(8,128)(2,1)S(1)} collective-permute-done((bf16[4,8,32,128]{3,2,1,0:T(8,128)(2,1)S(1)}, bf16[4,8,32,128]{3,2,1,0:T(8,128)(2,1)S(1)}, u32[]{:S(2)}, u32[]{:S(2)}) %collective-permute-start.39) | collective-permute-done | bytes 262176 | tf_op jit(solution)/shard_map/ppermute | solution.py:279
  498.0 5.6 %collective-permute-done.41 = bf16[4,8,32,128]{3,2,1,0:T(8,128)(2,1)S(1)} collective-permute-done((bf16[4,8,32,128]{3,2,1,0:T(8,128)(2,1)S(1)}, bf16[4,8,32,128]{3,2,1,0:T(8,128)(2,1)S(1)}, u32[]{:S(2)}, u32[]{:S(2)}) %collective-permute-start.41) | collective-permute-done | bytes 262176 | tf_op jit(solution)/shard_map/ppermute | solution.py:279
  505.3 4.3 collective-permute-start.43
  (198 shorter events, 91.1 us)
Async XLA Ops:
  66.0 130.5 %all-to-all-start.2 = ((bf16[8,16,4,8,256]{4,3,2,1,0:T(8,128)(2,1)}), bf16[8,16,4,8,256]{4,3,2,1,0:T(8,128)(2,1)S(1)}, u32[]{:S(2)}, u32[]{:S(2)}) async-start(bf16[8,16,4,8,256]{4,3,2,1,0:T(8,128)(2,1)} %get-tuple-element.42), calls=%async_computation.2 | async-start | bytes 4194304 | tf_op jit(solution)/shard_map/all_to_all | solution.py:284
  80.4 28.1 %collective-permute-start = (bf16[4,4,8,8,256]{4,3,2,1,0:T(8,128)(2,1)}, bf16[4,4,8,8,256]{4,3,2,1,0:T(8,128)(2,1)S(1)}, u32[]{:S(2)}, u32[]{:S(2)}) collective-permute-start(bf16[4,4,8,8,256]{4,3,2,1,0:T(8,128)(2,1)} %get-tuple-element.33), channel_id=1, source_target_pairs={{0,1},{1,0},{2,3},{3,2},{4,5},{5,4},{6,7},{7,6},{8,9},{9,8},{10,11... | collective-permute-start | bytes 1572872 | tf_op jit(solution)/shard_map/ppermute | solution.py:279
  81.0 28.3 %collective-permute-start.1 = (bf16[4,4,8,8,256]{4,3,2,1,0:T(8,128)(2,1)}, bf16[4,4,8,8,256]{4,3,2,1,0:T(8,128)(2,1)S(1)}, u32[]{:S(2)}, u32[]{:S(2)}) collective-permute-start(bf16[4,4,8,8,256]{4,3,2,1,0:T(8,128)(2,1)} %get-tuple-element.34), channel_id=1, source_target_pairs={{0,2},{1,3},{2,0},{3,1},{4,6},{5,7},{6,4},{7,5},{8,10},{9,11},{10,... | collective-permute-start | bytes 1572872 | tf_op jit(solution)/shard_map/ppermute | solution.py:279
  81.6 37.9 %collective-permute-start.2 = (bf16[4,4,8,8,256]{4,3,2,1,0:T(8,128)(2,1)}, bf16[4,4,8,8,256]{4,3,2,1,0:T(8,128)(2,1)S(1)}, u32[]{:S(2)}, u32[]{:S(2)}) collective-permute-start(bf16[4,4,8,8,256]{4,3,2,1,0:T(8,128)(2,1)} %get-tuple-element.35), channel_id=1, source_target_pairs={{0,3},{1,2},{2,1},{3,0},{4,7},{5,6},{6,5},{7,4},{8,11},{9,10},{10,... | collective-permute-start | bytes 1572872 | tf_op jit(solution)/shard_map/ppermute | solution.py:279
  120.5 19.9 %collective-permute-start.3 = (bf16[4,4,8,8,256]{4,3,2,1,0:T(8,128)(2,1)}, bf16[4,4,8,8,256]{4,3,2,1,0:T(8,128)(2,1)}, u32[]{:S(2)}, u32[]{:S(2)}) collective-permute-start(bf16[4,4,8,8,256]{4,3,2,1,0:T(8,128)(2,1)} %pad_maximum_fusion.3), channel_id=1, source_target_pairs={{0,4},{1,5},{2,6},{3,7},{4,0},{5,1},{6,2},{7,3},{8,12},{9,13},{10,... | collective-permute-start | bytes 1572872 | tf_op jit(solution)/shard_map/ppermute | solution.py:279
  121.9 35.6 %collective-permute-start.4 = (bf16[4,4,8,8,256]{4,3,2,1,0:T(8,128)(2,1)}, bf16[4,4,8,8,256]{4,3,2,1,0:T(8,128)(2,1)}, u32[]{:S(2)}, u32[]{:S(2)}) collective-permute-start(bf16[4,4,8,8,256]{4,3,2,1,0:T(8,128)(2,1)} %pad_maximum_fusion.4), channel_id=1, source_target_pairs={{0,8},{1,9},{2,10},{3,11},{4,12},{5,13},{6,14},{7,15},{8,0},{9,1},... | collective-permute-start | bytes 1572872 | tf_op jit(solution)/shard_map/ppermute | solution.py:279
  123.2 47.2 %collective-permute-start.5 = (bf16[4,4,8,8,256]{4,3,2,1,0:T(8,128)(2,1)}, bf16[4,4,8,8,256]{4,3,2,1,0:T(8,128)(2,1)}, u32[]{:S(2)}, u32[]{:S(2)}) collective-permute-start(bf16[4,4,8,8,256]{4,3,2,1,0:T(8,128)(2,1)} %pad_maximum_fusion.5), channel_id=1, source_target_pairs={{0,12},{1,13},{2,14},{3,15},{4,8},{5,9},{6,10},{7,11},{8,4},{9,5},... | collective-permute-start | bytes 1572872 | tf_op jit(solution)/shard_map/ppermute | solution.py:279
  197.9 129.3 %all-to-all-start.1 = ((bf16[8,16,4,8,256]{4,3,2,1,0:T(8,128)(2,1)}), bf16[8,16,4,8,256]{4,3,2,1,0:T(8,128)(2,1)S(1)}, u32[]{:S(2)}, u32[]{:S(2)}) async-start(bf16[8,16,4,8,256]{4,3,2,1,0:T(8,128)(2,1)} %get-tuple-element.37), calls=%async_computation.1 | async-start | bytes 4194304 | tf_op jit(solution)/shard_map/all_to_all | solution.py:284
  203.2 56.3 %collective-permute-start.13 = (bf16[4,4,8,8,256]{4,3,2,1,0:T(8,128)(2,1)}, bf16[4,4,8,8,256]{4,3,2,1,0:T(8,128)(2,1)}, u32[]{:S(2)}, u32[]{:S(2)}) collective-permute-start(bf16[4,4,8,8,256]{4,3,2,1,0:T(8,128)(2,1)} %get-tuple-element.39), channel_id=1, source_target_pairs={{0,4},{1,5},{2,6},{3,7},{4,0},{5,1},{6,2},{7,3},{8,12},{9,13},{10,... | collective-permute-start | bytes 1572872 | tf_op jit(solution)/shard_map/ppermute | solution.py:279
  203.7 56.8 %collective-permute-start.14 = (bf16[4,4,8,8,256]{4,3,2,1,0:T(8,128)(2,1)}, bf16[4,4,8,8,256]{4,3,2,1,0:T(8,128)(2,1)}, u32[]{:S(2)}, u32[]{:S(2)}) collective-permute-start(bf16[4,4,8,8,256]{4,3,2,1,0:T(8,128)(2,1)} %get-tuple-element.40), channel_id=1, source_target_pairs={{0,8},{1,9},{2,10},{3,11},{4,12},{5,13},{6,14},{7,15},{8,0},{9,1},... | collective-permute-start | bytes 1572872 | tf_op jit(solution)/shard_map/ppermute | solution.py:279
  203.8 69.9 %collective-permute-start.19 = (bf16[2,2,16,8,512]{4,3,2,1,0:T(8,128)(2,1)S(1)}, bf16[2,2,16,8,512]{4,3,2,1,0:T(8,128)(2,1)S(1)}, u32[]{:S(2)}, u32[]{:S(2)}) collective-permute-start(bf16[2,2,16,8,512]{4,3,2,1,0:T(8,128)(2,1)S(1)} %constant_dynamic-slice_fusion), channel_id=1, source_target_pairs={{0,8},{1,9},{2,10},{3,11},{4,12},{5,13},{6,14},{7,15},{8,0},{9,1},... | collective-permute-start | bytes 1572872 | tf_op jit(solution)/shard_map/ppermute | solution.py:279
  206.8 66.2 %collective-permute-start.15 = (bf16[4,4,8,8,256]{4,3,2,1,0:T(8,128)(2,1)}, bf16[4,4,8,8,256]{4,3,2,1,0:T(8,128)(2,1)S(1)}, u32[]{:S(2)}, u32[]{:S(2)}) collective-permute-start(bf16[4,4,8,8,256]{4,3,2,1,0:T(8,128)(2,1)} %get-tuple-element.41), channel_id=1, source_target_pairs={{0,12},{1,13},{2,14},{3,15},{4,8},{5,9},{6,10},{7,11},{8,4},{9,5},... | collective-permute-start | bytes 1572872 | tf_op jit(solution)/shard_map/ppermute | solution.py:279
  273.1 14.8 %collective-permute-start.16 = (bf16[4,4,8,8,256]{4,3,2,1,0:T(8,128)(2,1)S(1)}, bf16[4,4,8,8,256]{4,3,2,1,0:T(8,128)(2,1)S(1)}, u32[]{:S(2)}, u32[]{:S(2)}) collective-permute-start(bf16[4,4,8,8,256]{4,3,2,1,0:T(8,128)(2,1)S(1)} %pad_maximum_fusion.6), channel_id=1, source_target_pairs={{0,1},{1,0},{2,3},{3,2},{4,5},{5,4},{6,7},{7,6},{8,9},{9,8},{10,11... | collective-permute-start | bytes 1572872 | tf_op jit(solution)/shard_map/ppermute | solution.py:279
  273.8 25.6 %collective-permute-start.17 = (bf16[4,4,8,8,256]{4,3,2,1,0:T(8,128)(2,1)S(1)}, bf16[4,4,8,8,256]{4,3,2,1,0:T(8,128)(2,1)S(1)}, u32[]{:S(2)}, u32[]{:S(2)}) collective-permute-start(bf16[4,4,8,8,256]{4,3,2,1,0:T(8,128)(2,1)S(1)} %pad_maximum_fusion.7), channel_id=1, source_target_pairs={{0,2},{1,3},{2,0},{3,1},{4,6},{5,7},{6,4},{7,5},{8,10},{9,11},{10,... | collective-permute-start | bytes 1572872 | tf_op jit(solution)/shard_map/ppermute | solution.py:279
  274.5 24.9 %collective-permute-start.18 = (bf16[4,4,8,8,256]{4,3,2,1,0:T(8,128)(2,1)S(1)}, bf16[4,4,8,8,256]{4,3,2,1,0:T(8,128)(2,1)S(1)}, u32[]{:S(2)}, u32[]{:S(2)}) collective-permute-start(bf16[4,4,8,8,256]{4,3,2,1,0:T(8,128)(2,1)S(1)} %pad_maximum_fusion.8), channel_id=1, source_target_pairs={{0,3},{1,2},{2,1},{3,0},{4,7},{5,6},{6,5},{7,4},{8,11},{9,10},{10,... | collective-permute-start | bytes 1572872 | tf_op jit(solution)/shard_map/ppermute | solution.py:279
  328.4 87.2 %all-to-all-start.3 = ((bf16[8,16,4,8,256]{4,3,2,1,0:T(8,128)(2,1)}), bf16[8,16,4,8,256]{4,3,2,1,0:T(8,128)(2,1)}, u32[]{:S(2)}, u32[]{:S(2)}) async-start(bf16[8,16,4,8,256]{4,3,2,1,0:T(8,128)(2,1)} %get-tuple-element.43), calls=%async_computation.3 | async-start | bytes 4194304 | tf_op jit(solution)/shard_map/all_to_all | solution.py:284
  333.6 45.4 %collective-permute-start.27 = (bf16[4,4,8,8,256]{4,3,2,1,0:T(8,128)(2,1)}, bf16[4,4,8,8,256]{4,3,2,1,0:T(8,128)(2,1)S(1)}, u32[]{:S(2)}, u32[]{:S(2)}) collective-permute-start(bf16[4,4,8,8,256]{4,3,2,1,0:T(8,128)(2,1)} %get-tuple-element.50), channel_id=1, source_target_pairs={{0,4},{1,5},{2,6},{3,7},{4,0},{5,1},{6,2},{7,3},{8,12},{9,13},{10,... | collective-permute-start | bytes 1572872 | tf_op jit(solution)/shard_map/ppermute | solution.py:279
  334.4 49.9 %collective-permute-start.28 = (bf16[4,4,8,8,256]{4,3,2,1,0:T(8,128)(2,1)}, bf16[4,4,8,8,256]{4,3,2,1,0:T(8,128)(2,1)S(1)}, u32[]{:S(2)}, u32[]{:S(2)}) collective-permute-start(bf16[4,4,8,8,256]{4,3,2,1,0:T(8,128)(2,1)} %get-tuple-element.51), channel_id=1, source_target_pairs={{0,8},{1,9},{2,10},{3,11},{4,12},{5,13},{6,14},{7,15},{8,0},{9,1},... | collective-permute-start | bytes 1572872 | tf_op jit(solution)/shard_map/ppermute | solution.py:279
  336.6 47.7 %collective-permute-start.29 = (bf16[4,4,8,8,256]{4,3,2,1,0:T(8,128)(2,1)}, bf16[4,4,8,8,256]{4,3,2,1,0:T(8,128)(2,1)S(1)}, u32[]{:S(2)}, u32[]{:S(2)}) collective-permute-start(bf16[4,4,8,8,256]{4,3,2,1,0:T(8,128)(2,1)} %get-tuple-element.52), channel_id=1, source_target_pairs={{0,12},{1,13},{2,14},{3,15},{4,8},{5,9},{6,10},{7,11},{8,4},{9,5},... | collective-permute-start | bytes 1572872 | tf_op jit(solution)/shard_map/ppermute | solution.py:279
  340.8 70.2 %collective-permute-start.35 = (bf16[2,2,16,8,512]{4,3,2,1,0:T(8,128)(2,1)S(1)}, bf16[2,2,16,8,512]{4,3,2,1,0:T(8,128)(2,1)S(1)}, u32[]{:S(2)}, u32[]{:S(2)}) collective-permute-start(bf16[2,2,16,8,512]{4,3,2,1,0:T(8,128)(2,1)S(1)} %slice.334), channel_id=1, source_target_pairs={{0,16},{16,0},{1,17},{17,1},{2,18},{18,2},{3,19},{19,3},{4,20},{20... | collective-permute-start | bytes 1572872 | tf_op jit(solution)/shard_map/ppermute | solution.py:288
  340.9 47.4 %collective-permute-start.21 = (bf16[4,4,8,8,256]{4,3,2,1,0:T(8,128)(2,1)S(1)}, bf16[4,4,8,8,256]{4,3,2,1,0:T(8,128)(2,1)S(1)}, u32[]{:S(2)}, u32[]{:S(2)}) collective-permute-start(bf16[4,4,8,8,256]{4,3,2,1,0:T(8,128)(2,1)S(1)} %copy-done.22), channel_id=1, source_target_pairs={{0,1},{1,0},{2,3},{3,2},{4,5},{5,4},{6,7},{7,6},{8,9},{9,8},{10,11... | collective-permute-start | bytes 1572872 | tf_op jit(solution)/shard_map/ppermute | solution.py:279
  379.1 26.5 %collective-permute-start.22 = (bf16[4,4,8,8,256]{4,3,2,1,0:T(8,128)(2,1)S(1)}, bf16[4,4,8,8,256]{4,3,2,1,0:T(8,128)(2,1)S(1)}, u32[]{:S(2)}, u32[]{:S(2)}) collective-permute-start(bf16[4,4,8,8,256]{4,3,2,1,0:T(8,128)(2,1)S(1)} %copy-done.21), channel_id=1, source_target_pairs={{0,2},{1,3},{2,0},{3,1},{4,6},{5,7},{6,4},{7,5},{8,10},{9,11},{10,... | collective-permute-start | bytes 1572872 | tf_op jit(solution)/shard_map/ppermute | solution.py:279
  384.3 24.1 %collective-permute-start.23 = (bf16[4,4,8,8,256]{4,3,2,1,0:T(8,128)(2,1)S(1)}, bf16[4,4,8,8,256]{4,3,2,1,0:T(8,128)(2,1)S(1)}, u32[]{:S(2)}, u32[]{:S(2)}) collective-permute-start(bf16[4,4,8,8,256]{4,3,2,1,0:T(8,128)(2,1)S(1)} %copy-done.20), channel_id=1, source_target_pairs={{0,3},{1,2},{2,1},{3,0},{4,7},{5,6},{6,5},{7,4},{8,11},{9,10},{10,... | collective-permute-start | bytes 1572872 | tf_op jit(solution)/shard_map/ppermute | solution.py:279
  384.5 27.6 %collective-permute-start.30 = (bf16[4,4,8,8,256]{4,3,2,1,0:T(8,128)(2,1)S(1)}, bf16[4,4,8,8,256]{4,3,2,1,0:T(8,128)(2,1)S(1)}, u32[]{:S(2)}, u32[]{:S(2)}) collective-permute-start(bf16[4,4,8,8,256]{4,3,2,1,0:T(8,128)(2,1)S(1)} %pad_maximum_fusion.12), channel_id=1, source_target_pairs={{0,1},{1,0},{2,3},{3,2},{4,5},{5,4},{6,7},{7,6},{8,9},{9,8},{10,11... | collective-permute-start | bytes 1572872 | tf_op jit(solution)/shard_map/ppermute | solution.py:279
  388.3 38.0 %collective-permute-start.31 = (bf16[4,4,8,8,256]{4,3,2,1,0:T(8,128)(2,1)}, bf16[4,4,8,8,256]{4,3,2,1,0:T(8,128)(2,1)}, u32[]{:S(2)}, u32[]{:S(2)}) collective-permute-start(bf16[4,4,8,8,256]{4,3,2,1,0:T(8,128)(2,1)} %pad_maximum_fusion.13), channel_id=1, source_target_pairs={{0,2},{1,3},{2,0},{3,1},{4,6},{5,7},{6,4},{7,5},{8,10},{9,11},{10,... | collective-permute-start | bytes 1572872 | tf_op jit(solution)/shard_map/ppermute | solution.py:279
  405.6 20.8 %collective-permute-start.32 = (bf16[4,4,8,8,256]{4,3,2,1,0:T(8,128)(2,1)}, bf16[4,4,8,8,256]{4,3,2,1,0:T(8,128)(2,1)}, u32[]{:S(2)}, u32[]{:S(2)}) collective-permute-start(bf16[4,4,8,8,256]{4,3,2,1,0:T(8,128)(2,1)} %pad_maximum_fusion.14), channel_id=1, source_target_pairs={{0,3},{1,2},{2,1},{3,0},{4,7},{5,6},{6,5},{7,4},{8,11},{9,10},{10,... | collective-permute-start | bytes 1572872 | tf_op jit(solution)/shard_map/ppermute | solution.py:279
  409.4 20.8 %collective-permute-start.24 = (bf16[4,4,8,8,256]{4,3,2,1,0:T(8,128)(2,1)}, bf16[4,4,8,8,256]{4,3,2,1,0:T(8,128)(2,1)}, u32[]{:S(2)}, u32[]{:S(2)}) collective-permute-start(bf16[4,4,8,8,256]{4,3,2,1,0:T(8,128)(2,1)} %pad_maximum_fusion.9), channel_id=1, source_target_pairs={{0,4},{1,5},{2,6},{3,7},{4,0},{5,1},{6,2},{7,3},{8,12},{9,13},{10,... | collective-permute-start | bytes 1572872 | tf_op jit(solution)/shard_map/ppermute | solution.py:279
  411.0 45.0 %collective-permute-start.25 = (bf16[4,4,8,8,256]{4,3,2,1,0:T(8,128)(2,1)}, bf16[4,4,8,8,256]{4,3,2,1,0:T(8,128)(2,1)}, u32[]{:S(2)}, u32[]{:S(2)}) collective-permute-start(bf16[4,4,8,8,256]{4,3,2,1,0:T(8,128)(2,1)} %pad_maximum_fusion.10), channel_id=1, source_target_pairs={{0,8},{1,9},{2,10},{3,11},{4,12},{5,13},{6,14},{7,15},{8,0},{9,1},... | collective-permute-start | bytes 1572872 | tf_op jit(solution)/shard_map/ppermute | solution.py:279
  412.8 57.2 %collective-permute-start.26 = (bf16[4,4,8,8,256]{4,3,2,1,0:T(8,128)(2,1)S(1)}, bf16[4,4,8,8,256]{4,3,2,1,0:T(8,128)(2,1)}, u32[]{:S(2)}, u32[]{:S(2)}) collective-permute-start(bf16[4,4,8,8,256]{4,3,2,1,0:T(8,128)(2,1)S(1)} %pad_maximum_fusion.11), channel_id=1, source_target_pairs={{0,12},{1,13},{2,14},{3,15},{4,8},{5,9},{6,10},{7,11},{8,4},{9,5},... | collective-permute-start | bytes 1572872 | tf_op jit(solution)/shard_map/ppermute | solution.py:279
  426.3 56.3 %collective-permute-start.34 = (bf16[2,2,16,8,512]{4,3,2,1,0:T(8,128)(2,1)S(1)}, bf16[2,2,16,8,512]{4,3,2,1,0:T(8,128)(2,1)S(1)}, u32[]{:S(2)}, u32[]{:S(2)}) collective-permute-start(bf16[2,2,16,8,512]{4,3,2,1,0:T(8,128)(2,1)S(1)} %slice.335), channel_id=1, source_target_pairs={{0,16},{16,0},{1,17},{17,1},{2,18},{18,2},{3,19},{19,3},{4,20},{20... | collective-permute-start | bytes 1572872 | tf_op jit(solution)/shard_map/ppermute | solution.py:288
  426.4 56.2 %collective-permute-start.36 = (bf16[2,2,16,8,512]{4,3,2,1,0:T(8,128)(2,1)S(1)}, bf16[2,2,16,8,512]{4,3,2,1,0:T(8,128)(2,1)S(1)}, u32[]{:S(2)}, u32[]{:S(2)}) collective-permute-start(bf16[2,2,16,8,512]{4,3,2,1,0:T(8,128)(2,1)S(1)} %copy-done.7), channel_id=1, source_target_pairs={{0,8},{1,9},{2,10},{3,11},{4,12},{5,13},{6,14},{7,15},{8,0},{9,1},... | collective-permute-start | bytes 1572872 | tf_op jit(solution)/shard_map/ppermute | solution.py:279
  430.2 56.2 %collective-permute-start.38 = (bf16[16,8,32,128]{3,2,1,0:T(8,128)(2,1)}, bf16[16,8,32,128]{3,2,1,0:T(8,128)(2,1)}, u32[]{:S(2)}, u32[]{:S(2)}) collective-permute-start(bf16[16,8,32,128]{3,2,1,0:T(8,128)(2,1)} %fusion), channel_id=1, source_target_pairs={{0,16},{16,0},{1,17},{17,1},{2,18},{18,2},{3,19},{19,3},{4,20},{20... | collective-permute-start | bytes 3145736 | tf_op jit(solution)/shard_map/ppermute | solution.py:288
  (44 other events, 422.4 us)
where the time goes:
time: 522 us; the launch traced here: 518 us
  waiting for transfers between devices  289 us (55%)
  Pallas kernels  89.4 us (17%)
  starting transfers between devices  64 us (12%)
  blocking collectives  30 us (6%)
  local copies, waits for them, and re-layouts  28.9 us (6%)
  other arithmetic  15.1 us (3%)
    ppermute x38, waiting for transfers between devices, flip(): return lax.ppermute(value, 'feat', [(i, i ^ bits) for i in range(16)])  286 us
    pallas_call x2, Pallas kernels, local_halves(): call(functools.partial(middle_kernel, grouping[h]), (4,), [near_spec] * 4...  52.1 us
    ppermute x38, starting transfers between devices, flip(): return lax.ppermute(value, 'feat', [(i, i ^ bits) for i in range(16)])  45.9 us
    all_to_all x1, blocking collectives, spread(): lax.all_to_all(value, 'feat', 0, 0, axis_index_groups=groups, tiled=True)  30 us
    all_to_all x3, starting transfers between devices, spread(): lax.all_to_all(value, 'feat', 0, 0, axis_index_groups=groups, tiled=True)  17.1 us
    pallas_call x1, Pallas kernels, local_halves(): call(functools.partial(finish_kernel, grouping), (2, steps), ([near_spec]...  12.4 us
    pallas_call x1, Pallas kernels, local_halves(): call(token_kernel, (16 // STEP,), [pl.BlockSpec((8, STEP, 4, 8, TT), lamb...  10.7 us
  transfers between devices with their start and end apart: 49, of which 27 were waited for; matrix products, arithmetic and copies ran while one was open for 7% of the time, Pallas kernels for 16%

commit v1 on v0

--- a/solution.py
+++ b/solution.py
@@ -13,6 +13,9 @@
 TT = 256
 STEP = 4
 PAIR = 2
+
+GO = ("z", "xy")
+COME = ("z", "z")
 
 
 def gelu_tanh(value):
@@ -149,14 +152,14 @@
             outs[r >> 3][(who[0] & 7) ^ (r & 7), at] = y[32 * r : 32 * r + 32].reshape(4, 8, TT).astype(BF)
 
 
-def middle_kernel(grouping, who, *refs):
+def middle_kernel(go, come, who, *refs):
     x_near, x_far, tb, w_ref = refs[:4], refs[4:7], refs[7], refs[8]
-    fb_out, ta_out, g_ref = refs[9:13], refs[13], refs[14]
-    sg, tg = refs[15], refs[16]
+    fb_out, ta_out, g_ref = refs[9:13], refs[13:21], refs[21]
+    sg, tg = refs[22], refs[23]
     f = who[0]
 
-    def place(s):
-        return (s >> 2, s & 3) if grouping == "z" else (s & 3, s >> 2)
+    def place(s, first):
+        return (s >> 2, s & 3) if first == "z" else (s & 3, s >> 2)
 
     w2f = rows8([w_ref[0, 0, f ^ s] for s in range(16)])
     w2 = w2f.astype(BF)
@@ -168,7 +171,7 @@
         at = (f & 7) ^ q
         pieces = []
         for s in range(16):
-            i, j = place(s)
+            i, j = place(s, go)
             pieces.append(x_near[i][0, 0, at] if j == 0 else x_far[j - 1][i, 0, at])
         x = rows8(pieces).astype(BF)
         back = tb[at, :, 0].astype(F32).reshape(128, TT).astype(BF)
@@ -182,10 +185,10 @@
             0.7978845608028654 + (3 * 0.7978845608028654 * 0.044715) * vv
         )
         pre_grad = (hidden_grad * slope).astype(BF)
-        ta_out[at, :, 0] = dot(w3t, hidden).reshape(16, 8, TT).astype(BF)
+        ta_out[q][:, 0] = dot(w3t, hidden).reshape(16, 8, TT).astype(BF)
         fb = dot(w2, pre_grad)
         for s in range(16):
-            i, j = place(s)
+            i, j = place(s, come)
             fb_out[i][j, 0, at] = fb[8 * s : 8 * s + 8].astype(BF)
         s_now = dot(x, pre_grad, 1, 1)
         t_now = dot(back, hidden, 1, 1)
@@ -202,11 +205,11 @@
 
 
 def token_kernel(who, *refs):
-    pieces, og, a_ref, out, g_ref = refs[:2], refs[2], refs[3], refs[4], refs[5]
+    pieces, og, a_ref, out, g_ref = refs[:16], refs[16], refs[17], refs[18], refs[19]
     f, tok = who[0], who[1]
     for n in range(STEP):
         at = (f & (STEP - 1)) ^ n
-        parts = [pieces[r >> 3][(f & 7) ^ (r & 7), at] for r in range(16)]
+        parts = [piece[at] for piece in pieces]
         rows = jnp.concatenate([part.astype(F32).reshape(32, TT) for part in parts], axis=0).astype(BF)
         out[group_rows(at), :] = dot(gathered(who, a_ref, n), rows, 0, 0).astype(BF)
         g = compacted(dot(rows, og[group_rows(at), :], 1, 1))
@@ -303,8 +306,7 @@
     steps = tiles // PAIR
     f, tok = lax.axis_index("feat"), lax.axis_index("tok")
     who = jnp.stack([f, tok, f >> 3]).astype(jnp.int32)
-    grouping = ("xy", "z")
-    order = (1, 0)
+    order = (0, 1)
 
     a_one = first_weight.reshape(CB, width, 2, 64).transpose(3, 2, 0, 1).reshape(16, 32, width)
     a_four = fourth_weight.reshape(CB, 2, 64, width).transpose(2, 1, 0, 3).reshape(2, 8, 32, width)
@@ -325,14 +327,14 @@
     whole_a = pl.BlockSpec((16, 32, width), lambda t, w: (0, 0, 0))
     group = shape((4, 4, tiles, 8, TT))
     sent = call(
-        functools.partial(split_kernel, grouping), (steps,),
+        functools.partial(split_kernel, GO), (steps,),
         tile_specs + [whole_a],
         [pl.BlockSpec((4, 4, PAIR, 8, TT), lambda t, w: (0, 0, t, 0, 0))] * 8,
         [group] * 8,
         [pltpu.VMEM((512, 512), BF)],
         2 * 512 * 512 * tok_dev, 4 * 512 * tok_dev,
     )(who, inputs, inputs, a_one)
-    arrived = {h: two_stage(sent[4 * h : 4 * h + 4], grouping[h]) for h in order}
+    arrived = {h: two_stage(sent[4 * h : 4 * h + 4], GO[h]) for h in order}
 
     a_spec = pl.BlockSpec((2, STEP, 8, 32, width), lambda n, w: (0, n, 0, 0, 0))
     og_spec = pl.BlockSpec((512 * STEP, TT), lambda n, w: ((w[0] // STEP) ^ n, 0))
@@ -346,27 +348,28 @@
     results = {}
     near_spec = pl.BlockSpec((1, 1, tiles, 8, TT), lambda l, w: (0, l, 0, 0, 0))
     far_spec = pl.BlockSpec((4, 1, tiles, 8, TT), lambda l, w: (0, l, 0, 0, 0))
+    act_spec = pl.BlockSpec((16, 1, 8, TT), lambda l, w: (0, l, 0, 0))
     rows_spec = pl.BlockSpec((8, 16, 1, 8, TT), lambda l, w: (0, 0, l, 0, 0))
     for h in order:
         w_spec = pl.BlockSpec((1, 2, 16, 8, hidden), lambda l, w, h=h: (l ^ (2 * w[1] * h), 0, 0, 0, 0))
         g_spec = pl.BlockSpec((1, 2, 16, 8, hidden), lambda l, w: (l ^ (2 * w[1]), 0, 0, 0, 0))
         results[h] = call(
-            functools.partial(middle_kernel, grouping[h]), (4,),
+            functools.partial(middle_kernel, GO[h], COME[h]), (4,),
             [near_spec] * 4 + [far_spec] * 3 + [rows_spec, w_spec],
-            [far_spec] * 4 + [rows_spec, g_spec],
-            [group] * 4 + [shape((8, 16, 4, 8, TT))] + [shape((4, 2, 16, 8, hidden), F32)],
+            [far_spec] * 4 + [act_spec] * 8 + [g_spec],
+            [group] * 4 + [shape((16, 4, 8, TT))] * 8 + [shape((4, 2, 16, 8, hidden), F32)],
             [pltpu.VMEM((128, hidden), F32)] * 2,
             12 * 4 * 128 * hidden * tok_dev // 2, 20 * 2**20,
         )(who, *arrived[h], back[h], w_far if h else w_own)
-    returned = {h: two_stage(results[h][:4], grouping[h]) for h in order}
-    acts = {h: spread(results[h][4]) for h in order}
+    returned = {h: two_stage(results[h][:4], COME[h]) for h in order}
+    acts = {h: [results[h][4]] + [flip(results[h][4 + s], s) for s in range(1, 8)] for h in order}
 
     near_spec = pl.BlockSpec((1, 4, PAIR, 8, TT), lambda e, t, w: (0, 0, t, 0, 0))
     far_spec = pl.BlockSpec((4, 4, PAIR, 8, TT), lambda e, t, w: (0, 0, t, 0, 0))
     tile_spec = pl.BlockSpec((512, PAIR * TT), lambda e, t, w: (0, (w[2] ^ e) * steps + t))
     whole_a = pl.BlockSpec((16, 32, width), lambda e, t, w: (0, 0, 0))
     input_grad, first = call(
-        functools.partial(finish_kernel, grouping), (2, steps),
+        functools.partial(finish_kernel, COME), (2, steps),
         ([near_spec] * 4 + [far_spec] * 3) * 2 + [tile_spec, whole_a],
         [tile_spec, whole_a],
         [shape((512, tok_dev)), shape((16, 32, width), F32)],
@@ -376,18 +379,18 @@
 
     layer_out, fourth = call(
         token_kernel, (16 // STEP,),
-        [pl.BlockSpec((8, STEP, 4, 8, TT), lambda n, w: (0, (w[0] // STEP) ^ n, 0, 0, 0))] * 2 + [og_spec, a_spec],
+        [pl.BlockSpec((STEP, 4, 8, TT), lambda n, w: ((w[0] // STEP) ^ n, 0, 0, 0))] * 16 + [og_spec, a_spec],
         [og_spec, a_spec],
         [shape((8192, tok_part)), shape((2, 16, 8, 32, width), F32)], (),
         4 * 512 * 8192 * TT, 6 * 8192 * TT,
-    )(who, acts[0], acts[1], output_grad, a_all)
+    )(who, *acts[0], *acts[1], output_grad, a_all)
 
     def both(mine):
         other = swap(mine)
         low, high = jnp.where(tok == 0, mine, other), jnp.where(tok == 0, other, mine)
         return jnp.concatenate([low, high], axis=0)
 
-    kept = [results[h][5][:2] + swap(results[h][5][2:].astype(BF)).astype(F32) for h in (0, 1)]
+    kept = [results[h][12][:2] + swap(results[h][12][2:].astype(BF)).astype(F32) for h in (0, 1)]
     middle = both(kept[0] + flip(kept[1].astype(BF), 8).astype(F32)) * scale
     second = middle[:, 0].reshape(CB, 16, 2, CB, hidden).transpose(0, 2, 1, 3, 4).reshape(CB, width, hidden)
     third = middle[:, 1].reshape(CB, 16, 2, CB, hidden).transpose(0, 4, 2, 1, 3).reshape(CB, hidden, width)

time: 522 us -> 485 us (0.929)
  blocking collectives: 30 us -> 0 us
  starting transfers between devices: 64 us -> 88.5 us
  waiting for transfers between devices: 289 us -> 267 us
  other arithmetic: 15.1 us -> 6.7 us
    ppermute x38 -> x52, waiting for transfers between devices: 286 us -> 247 us  [flip(): return lax.ppermute(value, 'feat', [(i, i ^ bits) for i in range(16)])]
    ppermute x38 -> x52, starting transfers between devices: 45.9 us -> 76.7 us  [flip(): return lax.ppermute(value, 'feat', [(i, i ^ bits) for i in range(16)])]
    all_to_all x1 -> x0, blocking collectives: 30 us -> none  [spread(): lax.all_to_all(value, 'feat', 0, 0, axis_index_groups=groups, tiled=True)]
    all_to_all x3 -> x2, waiting for transfers between devices: 0.01 us -> 17.7 us  [spread(): lax.all_to_all(value, 'feat', 0, 0, axis_index_groups=groups, tiled=True)]
    all_to_all x3 -> x2, starting transfers between devices: 17.1 us -> 11 us  [spread(): lax.all_to_all(value, 'feat', 0, 0, axis_index_groups=groups, tiled=True)]
    another operation x12, other arithmetic: 6.54 us -> 0.83 us  [two_stage(): far = [flip(jnp.stack([n[j] for n in near]), two * j) for j in (1, 2, 3)]]
    unnamed x59 -> x107, local copies, waits for them, and re-layouts: 9.72 us -> 12.4 us
  transfers between devices with their start and end apart: 49 -> 62, of which waited for: 27 -> 29; matrix products, arithmetic and copies ran while one was open for 7% -> 4% of each run, Pallas kernels for 16% -> 17%
where the time goes in v1:
time: 485 us; the launch traced here: 481 us
  waiting for transfers between devices  267 us (55%)
  Pallas kernels  90.5 us (19%)
  starting transfers between devices  88.5 us (18%)
  local copies, waits for them, and re-layouts  26.6 us (5%)
  other arithmetic  6.7 us (1%)
    ppermute x52, waiting for transfers between devices, flip(): return lax.ppermute(value, 'feat', [(i, i ^ bits) for i in range(16)])  247 us
    ppermute x52, starting transfers between devices, flip(): return lax.ppermute(value, 'feat', [(i, i ^ bits) for i in range(16)])  76.7 us
    pallas_call x2, Pallas kernels, local_halves(): call(functools.partial(middle_kernel, GO[h], COME[h]), (4,), [near_spec]...  52.6 us
    all_to_all x2, waiting for transfers between devices, spread(): lax.all_to_all(value, 'feat', 0, 0, axis_index_groups=groups, tiled=True)  17.7 us
    pallas_call x1, Pallas kernels, local_halves(): call(functools.partial(finish_kernel, COME), (2, steps), ([near_spec] * 4...  12.6 us
    unnamed x107, local copies, waits for them, and re-layouts  12.4 us
    all_to_all x2, starting transfers between devices, spread(): lax.all_to_all(value, 'feat', 0, 0, axis_index_groups=groups, tiled=True)  11 us
    pallas_call x1, Pallas kernels, local_halves(): call(token_kernel, (16 // STEP,), [pl.BlockSpec((STEP, 4, 8, TT), lambda...  11 us
  transfers between devices with their start and end apart: 62, of which 29 were waited for; matrix products, arithmetic and copies ran while one was open for 4% of the time, Pallas kernels for 17%

profile of v1, /device:TPU:14, one launch (start us, length us, event | category | flops | bytes accessed | tf_op | source)
XLA Modules:
  0.0 481.4 jit_solution(8769596897606191859)
XLA Ops:
  5.8 3.1 collective-permute-done.8
  14.1 4.8 collective-permute-done.10
  20.2 4.1 collective-permute-done.11
  28.7 7.2 %shard_map.110 = (bf16[8,16,4,8,256]{4,3,2,1,0:T(8,128)(2,1)}, bf16[8,16,4,8,256]{4,3,2,1,0:T(8,128)(2,1)}) custom-call(s32[3]{0:T(128)} %pad_add_fusion.who, bf16[8192,256]{1,0:T(8,128)(2,1)} %refs_16_.1, bf16[2,16,8,32,128]{4,3,2,1,0:T(8,128)(2,1)} %pad_maximum_fusion.a_ref.refs_17_), custom_call_target="tpu_custom_call" | custom-call | flops 2147483648 | bytes 8388608 | tf_op jit(solution)/shard_map/pallas_call | solution.py:341
  35.9 5.8 %all-to-all-start.1 = ((bf16[8,16,4,8,256]{4,3,2,1,0:T(8,128)(2,1)}), bf16[8,16,4,8,256]{4,3,2,1,0:T(8,128)(2,1)S(1)}, u32[]{:S(2)}, u32[]{:S(2)}) async-start(bf16[8,16,4,8,256]{4,3,2,1,0:T(8,128)(2,1)} %get-tuple-element.63), calls=%async_computation.1 | async-start | bytes 4194304 | tf_op jit(solution)/shard_map/all_to_all | solution.py:287
  42.6 7.1 %shard_map.109 = (bf16[4,4,8,8,256]{4,3,2,1,0:T(8,128)(2,1)}, bf16[4,4,8,8,256]{4,3,2,1,0:T(8,128)(2,1)}, bf16[4,4,8,8,256]{4,3,2,1,0:T(8,128)(2,1)}, bf16[4,4,8...) custom-call(s32[3]{0:T(128)} %pad_add_fusion.who, ...), custom_call_target="tpu_custom_call" | custom-call | flops 2147483648 | bytes 8388608 | tf_op jit(solution)/shard_map/pallas_call | solution.py:329
  50.8 17.7 %all-to-all-done.1.refs_7_ = bf16[8,16,4,8,256]{4,3,2,1,0:T(8,128)(2,1)S(1)} async-done(((bf16[8,16,4,8,256]{4,3,2,1,0:T(8,128)(2,1)}), bf16[8,16,4,8,256]{4,3,2,1,0:T(8,128)(2,1)S(1)}, u32[]{:S(2)}, u32[]{:S(2)}) %all-to-all-start.1) | async-done | bytes 2097184 | tf_op jit(solution)/shard_map/all_to_all | solution.py:287
  69.8 5.2 %all-to-all-start = ((bf16[8,16,4,8,256]{4,3,2,1,0:T(8,128)(2,1)}), bf16[8,16,4,8,256]{4,3,2,1,0:T(8,128)(2,1)S(1)}, u32[]{:S(2)}, u32[]{:S(2)}) async-start(bf16[8,16,4,8,256]{4,3,2,1,0:T(8,128)(2,1)} %get-tuple-element.50), calls=%async_computation | async-start | bytes 4194304 | tf_op jit(solution)/shard_map/all_to_all | solution.py:287
  86.0 33.9 %collective-permute-done.21.refs_2_ = bf16[4,4,8,8,256]{4,3,2,1,0:T(8,128)(2,1)S(1)} collective-permute-done((bf16[4,4,8,8,256]{4,3,2,1,0:T(8,128)(2,1)}, bf16[4,4,8,8,256]{4,3,2,1,0:T(8,128)(2,1)S(1)}, u32[]{:S(2)}, u32[]{:S(2)}) %collective-permute-start.21) | collective-permute-done | bytes 524320 | tf_op jit(solution)/shard_map/ppermute | solution.py:282
  123.2 20.4 %collective-permute-done.refs_1_ = bf16[4,4,8,8,256]{4,3,2,1,0:T(8,128)(2,1)S(1)} collective-permute-done((bf16[4,4,8,8,256]{4,3,2,1,0:T(8,128)(2,1)}, bf16[4,4,8,8,256]{4,3,2,1,0:T(8,128)(2,1)S(1)}, u32[]{:S(2)}, u32[]{:S(2)}) %collective-permute-start) | collective-permute-done | bytes 524320 | tf_op jit(solution)/shard_map/ppermute | solution.py:282
  148.8 8.2 %collective-permute-done.2.refs_3_ = bf16[4,4,8,8,256]{4,3,2,1,0:T(8,128)(2,1)S(1)} collective-permute-done((bf16[4,4,8,8,256]{4,3,2,1,0:T(8,128)(2,1)S(1)}, bf16[4,4,8,8,256]{4,3,2,1,0:T(8,128)(2,1)S(1)}, u32[]{:S(2)}, u32[]{:S(2)}) %collective-permute-start.2) | collective-permute-done | bytes 524320 | tf_op jit(solution)/shard_map/ppermute | solution.py:282
  162.0 24.8 %collective-permute-done.24.refs_5_ = bf16[4,4,8,8,256]{4,3,2,1,0:T(8,128)(2,1)S(1)} collective-permute-done((bf16[4,4,8,8,256]{4,3,2,1,0:T(8,128)(2,1)S(1)}, bf16[4,4,8,8,256]{4,3,2,1,0:T(8,128)(2,1)S(1)}, u32[]{:S(2)}, u32[]{:S(2)}) %collective-permute-start.24) | collective-permute-done | bytes 524320 | tf_op jit(solution)/shard_map/ppermute | solution.py:282
  187.6 12.1 %collective-permute-done.25.refs_6_ = bf16[4,4,8,8,256]{4,3,2,1,0:T(8,128)(2,1)} collective-permute-done((bf16[4,4,8,8,256]{4,3,2,1,0:T(8,128)(2,1)S(1)}, bf16[4,4,8,8,256]{4,3,2,1,0:T(8,128)(2,1)}, u32[]{:S(2)}, u32[]{:S(2)}) %collective-permute-start.25) | collective-permute-done | bytes 524320 | tf_op jit(solution)/shard_map/ppermute | solution.py:282
  199.7 26.2 %shard_map.112 = (bf16[4,4,8,8,256]{4,3,2,1,0:T(8,128)(2,1)}, bf16[4,4,8,8,256]{4,3,2,1,0:T(8,128)(2,1)}, bf16[4,4,8,8,256]{4,3,2,1,0:T(8,128)(2,1)}, bf16[4,4,8...) custom-call(s32[3]{0:T(128)} %pad_add_fusion.who, ...), custom_call_target="tpu_custom_call" | custom-call | flops 6442450944 | bytes 20971520 | tf_op jit(solution)/shard_map/pallas_call | solution.py:356
  233.2 26.4 %shard_map.111 = (bf16[4,4,8,8,256]{4,3,2,1,0:T(8,128)(2,1)}, bf16[4,4,8,8,256]{4,3,2,1,0:T(8,128)(2,1)}, bf16[4,4,8,8,256]{4,3,2,1,0:T(8,128)(2,1)}, bf16[4,4,8...) custom-call(s32[3]{0:T(128)} %pad_add_fusion.who, ...), custom_call_target="tpu_custom_call" | custom-call | flops 6442450944 | bytes 20971520 | tf_op jit(solution)/shard_map/pallas_call | solution.py:356
  260.6 3.3 collective-permute-start.34
  270.2 6.5 %collective-permute-done.34.refs_15_ = bf16[16,4,8,256]{3,2,1,0:T(8,128)(2,1)S(1)} collective-permute-done((bf16[16,4,8,256]{3,2,1,0:T(8,128)(2,1)S(1)}, bf16[16,4,8,256]{3,2,1,0:T(8,128)(2,1)S(1)}, u32[]{:S(2)}, u32[]{:S(2)}) %collective-permute-start.34) | collective-permute-done | bytes 262176 | tf_op jit(solution)/shard_map/ppermute | solution.py:282
  281.5 6.9 %collective-permute-start.19 = (bf16[16,4,8,256]{3,2,1,0:T(8,128)(2,1)}, bf16[16,4,8,256]{3,2,1,0:T(8,128)(2,1)S(1)}, u32[]{:S(2)}, u32[]{:S(2)}) collective-permute-start(bf16[16,4,8,256]{3,2,1,0:T(8,128)(2,1)} %get-tuple-element.58), channel_id=1, source_target_pairs={{0,7},{1,6},{2,5},{3,4},{4,3},{5,2},{6,1},{7,0},{8,15},{9,14},{10,... | collective-permute-start | bytes 786440 | tf_op jit(solution)/shard_map/ppermute | solution.py:282
  292.9 6.0 %collective-permute-done.19.refs_7_ = bf16[16,4,8,256]{3,2,1,0:T(8,128)(2,1)S(1)} collective-permute-done((bf16[16,4,8,256]{3,2,1,0:T(8,128)(2,1)}, bf16[16,4,8,256]{3,2,1,0:T(8,128)(2,1)S(1)}, u32[]{:S(2)}, u32[]{:S(2)}) %collective-permute-start.19) | collective-permute-done | bytes 262176 | tf_op jit(solution)/shard_map/ppermute | solution.py:282
  299.6 11.0 %shard_map.113 = (bf16[8192,256]{1,0:T(8,128)(2,1)}, f32[2,16,8,32,128]{4,3,2,1,0:T(8,128)}) custom-call(s32[3]{0:T(128)} %pad_add_fusion.who, bf16[16,4,8,256]{3,2,1,0:T(8,128)(2,1)} %get-tuple-element.51.refs_0_, bf16[16,4,8,256]{3,2,1,0:T(8,128)(2,1)} %copy-done.44, bf16[16,4,8,256]{3,2,1,0:T(8,128)(2,1)} %copy-done.45, ...), custom_call_target="tpu_custom_call" | custom-call | flops 4294967296 | bytes 12582912 | tf_op jit(solution)/shard_map/pallas_call | solution.py:380
  312.6 2.9 collective-permute-done.41.refs_8_
  315.4 9.3 %collective-permute-start.35 = (bf16[4,4,8,8,256]{4,3,2,1,0:T(8,128)(2,1)S(1)}, bf16[4,4,8,8,256]{4,3,2,1,0:T(8,128)(2,1)S(1)}, u32[]{:S(2)}, u32[]{:S(2)}) collective-permute-start(bf16[4,4,8,8,256]{4,3,2,1,0:T(8,128)(2,1)S(1)} %copy-done.25), channel_id=1, source_target_pairs={{0,4},{1,5},{2,6},{3,7},{4,0},{5,1},{6,2},{7,3},{8,12},{9,13},{10,... | collective-permute-start | bytes 1572872 | tf_op jit(solution)/shard_map/ppermute | solution.py:282
  325.5 7.6 %collective-permute-start.37 = (bf16[4,4,8,8,256]{4,3,2,1,0:T(8,128)(2,1)S(1)}, bf16[4,4,8,8,256]{4,3,2,1,0:T(8,128)(2,1)S(1)}, u32[]{:S(2)}, u32[]{:S(2)}) collective-permute-start(bf16[4,4,8,8,256]{4,3,2,1,0:T(8,128)(2,1)S(1)} %copy-done.22), channel_id=1, source_target_pairs={{0,12},{1,13},{2,14},{3,15},{4,8},{5,9},{6,10},{7,11},{8,4},{9,5},... | collective-permute-start | bytes 1572872 | tf_op jit(solution)/shard_map/ppermute | solution.py:282
  333.3 30.6 %collective-permute-done.43.refs_10_ = bf16[4,4,8,8,256]{4,3,2,1,0:T(8,128)(2,1)} collective-permute-done((bf16[4,4,8,8,256]{4,3,2,1,0:T(8,128)(2,1)}, bf16[4,4,8,8,256]{4,3,2,1,0:T(8,128)(2,1)}, u32[]{:S(2)}, u32[]{:S(2)}) %collective-permute-start.43) | collective-permute-done | bytes 524320 | tf_op jit(solution)/shard_map/ppermute | solution.py:282
  365.3 18.6 %collective-permute-done.36.refs_2_ = bf16[4,4,8,8,256]{4,3,2,1,0:T(8,128)(2,1)S(1)} collective-permute-done((bf16[4,4,8,8,256]{4,3,2,1,0:T(8,128)(2,1)S(1)}, bf16[4,4,8,8,256]{4,3,2,1,0:T(8,128)(2,1)S(1)}, u32[]{:S(2)}, u32[]{:S(2)}) %collective-permute-start.36) | collective-permute-done | bytes 524320 | tf_op jit(solution)/shard_map/ppermute | solution.py:282
  385.6 11.9 %collective-permute-done.37.refs_3_ = bf16[4,4,8,8,256]{4,3,2,1,0:T(8,128)(2,1)S(1)} collective-permute-done((bf16[4,4,8,8,256]{4,3,2,1,0:T(8,128)(2,1)S(1)}, bf16[4,4,8,8,256]{4,3,2,1,0:T(8,128)(2,1)S(1)}, u32[]{:S(2)}, u32[]{:S(2)}) %collective-permute-start.37) | collective-permute-done | bytes 524320 | tf_op jit(solution)/shard_map/ppermute | solution.py:282
  402.6 3.2 collective-permute-done.50
  409.3 3.7 collective-permute-done.55
  414.2 11.5 %collective-permute-done.54 = bf16[4,8,32,128]{3,2,1,0:T(8,128)(2,1)S(1)} collective-permute-done((bf16[4,8,32,128]{3,2,1,0:T(8,128)(2,1)S(1)}, bf16[4,8,32,128]{3,2,1,0:T(8,128)(2,1)S(1)}, u32[]{:S(2)}, u32[]{:S(2)}) %collective-permute-start.54) | collective-permute-done | bytes 262176 | tf_op jit(solution)/shard_map/ppermute | solution.py:282
  427.9 20.4 %collective-permute-done.45.refs_12_ = bf16[4,4,8,8,256]{4,3,2,1,0:T(8,128)(2,1)S(1)} collective-permute-done((bf16[4,4,8,8,256]{4,3,2,1,0:T(8,128)(2,1)S(1)}, bf16[4,4,8,8,256]{4,3,2,1,0:T(8,128)(2,1)S(1)}, u32[]{:S(2)}, u32[]{:S(2)}) %collective-permute-start.45) | collective-permute-done | bytes 524320 | tf_op jit(solution)/shard_map/ppermute | solution.py:282
  448.9 8.7 %collective-permute-done.39.refs_5_ = bf16[4,4,8,8,256]{4,3,2,1,0:T(8,128)(2,1)S(1)} collective-permute-done((bf16[4,4,8,8,256]{4,3,2,1,0:T(8,128)(2,1)S(1)}, bf16[4,4,8,8,256]{4,3,2,1,0:T(8,128)(2,1)S(1)}, u32[]{:S(2)}, u32[]{:S(2)}) %collective-permute-start.39) | collective-permute-done | bytes 524320 | tf_op jit(solution)/shard_map/ppermute | solution.py:282
  459.3 12.6 %shard_map.114 = (bf16[512,4096]{1,0:T(8,128)(2,1)}, f32[16,32,128]{2,1,0:T(8,128)}) custom-call(s32[3]{0:T(128)} %pad_add_fusion.who, bf16[4,4,8,8,256]{4,3,2,1,0:T(8,128)(2,1)} %get-tuple-element.73.refs_0_, bf16[4,4,8,8,256]{4,3,2,1,0:T(8,128)(2,1)} %copy-done.12, bf16[4,4,8,8,256]{4,3,2,1,0:T(8,128)(2,1)} %copy-done.14, ...), custom_call_target="tpu_custom_call" | custom-call | flops 4294967296 | bytes 12582912 | tf_op jit(solution)/shard_map/pallas_call | solution.py:371
  (271 shorter events, 98.5 us)
Async XLA Ops:
  35.9 32.6 %all-to-all-start.1 = ((bf16[8,16,4,8,256]{4,3,2,1,0:T(8,128)(2,1)}), bf16[8,16,4,8,256]{4,3,2,1,0:T(8,128)(2,1)S(1)}, u32[]{:S(2)}, u32[]{:S(2)}) async-start(bf16[8,16,4,8,256]{4,3,2,1,0:T(8,128)(2,1)} %get-tuple-element.63), calls=%async_computation.1 | async-start | bytes 4194304 | tf_op jit(solution)/shard_map/all_to_all | solution.py:287
  49.7 34.9 %collective-permute-start.20 = (bf16[4,4,8,8,256]{4,3,2,1,0:T(8,128)(2,1)}, bf16[4,4,8,8,256]{4,3,2,1,0:T(8,128)(2,1)}, u32[]{:S(2)}, u32[]{:S(2)}) collective-permute-start(bf16[4,4,8,8,256]{4,3,2,1,0:T(8,128)(2,1)} %get-tuple-element.60), channel_id=1, source_target_pairs={{0,1},{1,0},{2,3},{3,2},{4,5},{5,4},{6,7},{7,6},{8,9},{9,8},{10,11... | collective-permute-start | bytes 1572872 | tf_op jit(solution)/shard_map/ppermute | solution.py:282
  69.8 162.1 %all-to-all-start = ((bf16[8,16,4,8,256]{4,3,2,1,0:T(8,128)(2,1)}), bf16[8,16,4,8,256]{4,3,2,1,0:T(8,128)(2,1)S(1)}, u32[]{:S(2)}, u32[]{:S(2)}) async-start(bf16[8,16,4,8,256]{4,3,2,1,0:T(8,128)(2,1)} %get-tuple-element.50), calls=%async_computation | async-start | bytes 4194304 | tf_op jit(solution)/shard_map/all_to_all | solution.py:287
  78.5 68.0 %collective-permute-start.26 = (bf16[2,2,16,8,512]{4,3,2,1,0:T(8,128)(2,1)S(1)}, bf16[2,2,16,8,512]{4,3,2,1,0:T(8,128)(2,1)S(1)}, u32[]{:S(2)}, u32[]{:S(2)}) collective-permute-start(bf16[2,2,16,8,512]{4,3,2,1,0:T(8,128)(2,1)S(1)} %constant_dynamic-slice_fusion), channel_id=1, source_target_pairs={{0,8},{1,9},{2,10},{3,11},{4,12},{5,13},{6,14},{7,15},{8,0},{9,1},... | collective-permute-start | bytes 1572872 | tf_op jit(solution)/shard_map/ppermute | solution.py:282
  80.1 63.5 %collective-permute-start = (bf16[4,4,8,8,256]{4,3,2,1,0:T(8,128)(2,1)}, bf16[4,4,8,8,256]{4,3,2,1,0:T(8,128)(2,1)S(1)}, u32[]{:S(2)}, u32[]{:S(2)}) collective-permute-start(bf16[4,4,8,8,256]{4,3,2,1,0:T(8,128)(2,1)} %get-tuple-element.47), channel_id=1, source_target_pairs={{0,4},{1,5},{2,6},{3,7},{4,0},{5,1},{6,2},{7,3},{8,12},{9,13},{10,... | collective-permute-start | bytes 1572872 | tf_op jit(solution)/shard_map/ppermute | solution.py:282
  80.6 39.2 %collective-permute-start.21 = (bf16[4,4,8,8,256]{4,3,2,1,0:T(8,128)(2,1)}, bf16[4,4,8,8,256]{4,3,2,1,0:T(8,128)(2,1)S(1)}, u32[]{:S(2)}, u32[]{:S(2)}) collective-permute-start(bf16[4,4,8,8,256]{4,3,2,1,0:T(8,128)(2,1)} %get-tuple-element.61), channel_id=1, source_target_pairs={{0,2},{1,3},{2,0},{3,1},{4,6},{5,7},{6,4},{7,5},{8,10},{9,11},{10,... | collective-permute-start | bytes 1572872 | tf_op jit(solution)/shard_map/ppermute | solution.py:282
  81.2 39.5 %collective-permute-start.22 = (bf16[4,4,8,8,256]{4,3,2,1,0:T(8,128)(2,1)}, bf16[4,4,8,8,256]{4,3,2,1,0:T(8,128)(2,1)S(1)}, u32[]{:S(2)}, u32[]{:S(2)}) collective-permute-start(bf16[4,4,8,8,256]{4,3,2,1,0:T(8,128)(2,1)} %get-tuple-element.62), channel_id=1, source_target_pairs={{0,3},{1,2},{2,1},{3,0},{4,7},{5,6},{6,5},{7,4},{8,11},{9,10},{10,... | collective-permute-start | bytes 1572872 | tf_op jit(solution)/shard_map/ppermute | solution.py:282
  84.6 63.4 %collective-permute-start.1 = (bf16[4,4,8,8,256]{4,3,2,1,0:T(8,128)(2,1)S(1)}, bf16[4,4,8,8,256]{4,3,2,1,0:T(8,128)(2,1)S(1)}, u32[]{:S(2)}, u32[]{:S(2)}) collective-permute-start(bf16[4,4,8,8,256]{4,3,2,1,0:T(8,128)(2,1)S(1)} %copy-done.28), channel_id=1, source_target_pairs={{0,8},{1,9},{2,10},{3,11},{4,12},{5,13},{6,14},{7,15},{8,0},{9,1},... | collective-permute-start | bytes 1572872 | tf_op jit(solution)/shard_map/ppermute | solution.py:282
  119.9 37.2 %collective-permute-start.2 = (bf16[4,4,8,8,256]{4,3,2,1,0:T(8,128)(2,1)S(1)}, bf16[4,4,8,8,256]{4,3,2,1,0:T(8,128)(2,1)S(1)}, u32[]{:S(2)}, u32[]{:S(2)}) collective-permute-start(bf16[4,4,8,8,256]{4,3,2,1,0:T(8,128)(2,1)S(1)} %copy-done.27), channel_id=1, source_target_pairs={{0,12},{1,13},{2,14},{3,15},{4,8},{5,9},{6,10},{7,11},{8,4},{9,5},... | collective-permute-start | bytes 1572872 | tf_op jit(solution)/shard_map/ppermute | solution.py:282
  120.8 39.1 %collective-permute-start.23 = (bf16[4,4,8,8,256]{4,3,2,1,0:T(8,128)(2,1)S(1)}, bf16[4,4,8,8,256]{4,3,2,1,0:T(8,128)(2,1)S(1)}, u32[]{:S(2)}, u32[]{:S(2)}) collective-permute-start(bf16[4,4,8,8,256]{4,3,2,1,0:T(8,128)(2,1)S(1)} %pad_maximum_fusion.6), channel_id=1, source_target_pairs={{0,4},{1,5},{2,6},{3,7},{4,0},{5,1},{6,2},{7,3},{8,12},{9,13},{10,... | collective-permute-start | bytes 1572872 | tf_op jit(solution)/shard_map/ppermute | solution.py:282
  143.6 43.2 %collective-permute-start.24 = (bf16[4,4,8,8,256]{4,3,2,1,0:T(8,128)(2,1)S(1)}, bf16[4,4,8,8,256]{4,3,2,1,0:T(8,128)(2,1)S(1)}, u32[]{:S(2)}, u32[]{:S(2)}) collective-permute-start(bf16[4,4,8,8,256]{4,3,2,1,0:T(8,128)(2,1)S(1)} %pad_maximum_fusion.7), channel_id=1, source_target_pairs={{0,8},{1,9},{2,10},{3,11},{4,12},{5,13},{6,14},{7,15},{8,0},{9,1},... | collective-permute-start | bytes 1572872 | tf_op jit(solution)/shard_map/ppermute | solution.py:282
  146.5 53.2 %collective-permute-start.25 = (bf16[4,4,8,8,256]{4,3,2,1,0:T(8,128)(2,1)S(1)}, bf16[4,4,8,8,256]{4,3,2,1,0:T(8,128)(2,1)}, u32[]{:S(2)}, u32[]{:S(2)}) collective-permute-start(bf16[4,4,8,8,256]{4,3,2,1,0:T(8,128)(2,1)S(1)} %pad_maximum_fusion.8), channel_id=1, source_target_pairs={{0,12},{1,13},{2,14},{3,15},{4,8},{5,9},{6,10},{7,11},{8,4},{9,5},... | collective-permute-start | bytes 1572872 | tf_op jit(solution)/shard_map/ppermute | solution.py:282
  157.1 69.9 %collective-permute-start.3 = (bf16[4,4,8,8,256]{4,3,2,1,0:T(8,128)(2,1)S(1)}, bf16[4,4,8,8,256]{4,3,2,1,0:T(8,128)(2,1)S(1)}, u32[]{:S(2)}, u32[]{:S(2)}) collective-permute-start(bf16[4,4,8,8,256]{4,3,2,1,0:T(8,128)(2,1)S(1)} %pad_maximum_fusion.3), channel_id=1, source_target_pairs={{0,1},{1,0},{2,3},{3,2},{4,5},{5,4},{6,7},{7,6},{8,9},{9,8},{10,11... | collective-permute-start | bytes 1572872 | tf_op jit(solution)/shard_map/ppermute | solution.py:282
  158.0 71.4 %collective-permute-start.4 = (bf16[4,4,8,8,256]{4,3,2,1,0:T(8,128)(2,1)S(1)}, bf16[4,4,8,8,256]{4,3,2,1,0:T(8,128)(2,1)S(1)}, u32[]{:S(2)}, u32[]{:S(2)}) collective-permute-start(bf16[4,4,8,8,256]{4,3,2,1,0:T(8,128)(2,1)S(1)} %pad_maximum_fusion.4), channel_id=1, source_target_pairs={{0,2},{1,3},{2,0},{3,1},{4,6},{5,7},{6,4},{7,5},{8,10},{9,11},{10,... | collective-permute-start | bytes 1572872 | tf_op jit(solution)/shard_map/ppermute | solution.py:282
  160.0 69.5 %collective-permute-start.5 = (bf16[4,4,8,8,256]{4,3,2,1,0:T(8,128)(2,1)S(1)}, bf16[4,4,8,8,256]{4,3,2,1,0:T(8,128)(2,1)S(1)}, u32[]{:S(2)}, u32[]{:S(2)}) collective-permute-start(bf16[4,4,8,8,256]{4,3,2,1,0:T(8,128)(2,1)S(1)} %pad_maximum_fusion.5), channel_id=1, source_target_pairs={{0,3},{1,2},{2,1},{3,0},{4,7},{5,6},{6,5},{7,4},{8,11},{9,10},{10,... | collective-permute-start | bytes 1572872 | tf_op jit(solution)/shard_map/ppermute | solution.py:282
  225.8 33.7 %collective-permute-start.28 = (bf16[16,4,8,256]{3,2,1,0:T(8,128)(2,1)}, bf16[16,4,8,256]{3,2,1,0:T(8,128)(2,1)S(1)}, u32[]{:S(2)}, u32[]{:S(2)}) collective-permute-start(bf16[16,4,8,256]{3,2,1,0:T(8,128)(2,1)} %get-tuple-element.65), channel_id=1, source_target_pairs={{0,1},{1,0},{2,3},{3,2},{4,5},{5,4},{6,7},{7,6},{8,9},{9,8},{10,11... | collective-permute-start | bytes 786440 | tf_op jit(solution)/shard_map/ppermute | solution.py:282
  226.1 34.5 %collective-permute-start.29 = (bf16[16,4,8,256]{3,2,1,0:T(8,128)(2,1)}, bf16[16,4,8,256]{3,2,1,0:T(8,128)(2,1)}, u32[]{:S(2)}, u32[]{:S(2)}) collective-permute-start(bf16[16,4,8,256]{3,2,1,0:T(8,128)(2,1)} %get-tuple-element.66), channel_id=1, source_target_pairs={{0,2},{1,3},{2,0},{3,1},{4,6},{5,7},{6,4},{7,5},{8,10},{9,11},{10,... | collective-permute-start | bytes 786440 | tf_op jit(solution)/shard_map/ppermute | solution.py:282
  227.1 36.8 %collective-permute-start.30 = (bf16[16,4,8,256]{3,2,1,0:T(8,128)(2,1)}, bf16[16,4,8,256]{3,2,1,0:T(8,128)(2,1)}, u32[]{:S(2)}, u32[]{:S(2)}) collective-permute-start(bf16[16,4,8,256]{3,2,1,0:T(8,128)(2,1)} %get-tuple-element.67), channel_id=1, source_target_pairs={{0,3},{1,2},{2,1},{3,0},{4,7},{5,6},{6,5},{7,4},{8,11},{9,10},{10,... | collective-permute-start | bytes 786440 | tf_op jit(solution)/shard_map/ppermute | solution.py:282
  229.4 34.7 %collective-permute-start.31 = (bf16[16,4,8,256]{3,2,1,0:T(8,128)(2,1)}, bf16[16,4,8,256]{3,2,1,0:T(8,128)(2,1)}, u32[]{:S(2)}, u32[]{:S(2)}) collective-permute-start(bf16[16,4,8,256]{3,2,1,0:T(8,128)(2,1)} %get-tuple-element.68), channel_id=1, source_target_pairs={{0,4},{1,5},{2,6},{3,7},{4,0},{5,1},{6,2},{7,3},{8,12},{9,13},{10,... | collective-permute-start | bytes 786440 | tf_op jit(solution)/shard_map/ppermute | solution.py:282
  230.3 34.8 %collective-permute-start.32 = (bf16[16,4,8,256]{3,2,1,0:T(8,128)(2,1)}, bf16[16,4,8,256]{3,2,1,0:T(8,128)(2,1)}, u32[]{:S(2)}, u32[]{:S(2)}) collective-permute-start(bf16[16,4,8,256]{3,2,1,0:T(8,128)(2,1)} %get-tuple-element.69), channel_id=1, source_target_pairs={{0,5},{1,4},{2,7},{3,6},{4,1},{5,0},{6,3},{7,2},{8,13},{9,12},{10,... | collective-permute-start | bytes 786440 | tf_op jit(solution)/shard_map/ppermute | solution.py:282
  289.9 111.4 %collective-permute-start.48 = (bf16[2,2,16,8,512]{4,3,2,1,0:T(8,128)(2,1)S(1)}, bf16[2,2,16,8,512]{4,3,2,1,0:T(8,128)(2,1)S(1)}, u32[]{:S(2)}, u32[]{:S(2)}) collective-permute-start(bf16[2,2,16,8,512]{4,3,2,1,0:T(8,128)(2,1)S(1)} %slice.335), channel_id=1, source_target_pairs={{0,16},{16,0},{1,17},{17,1},{2,18},{18,2},{3,19},{19,3},{4,20},{20... | collective-permute-start | bytes 1572872 | tf_op jit(solution)/shard_map/ppermute | solution.py:291
  290.6 35.0 %collective-permute-start.49 = (bf16[2,2,16,8,512]{4,3,2,1,0:T(8,128)(2,1)S(1)}, bf16[2,2,16,8,512]{4,3,2,1,0:T(8,128)(2,1)S(1)}, u32[]{:S(2)}, u32[]{:S(2)}) collective-permute-start(bf16[2,2,16,8,512]{4,3,2,1,0:T(8,128)(2,1)S(1)} %slice.334), channel_id=1, source_target_pairs={{0,16},{16,0},{1,17},{17,1},{2,18},{18,2},{3,19},{19,3},{4,20},{20... | collective-permute-start | bytes 1572872 | tf_op jit(solution)/shard_map/ppermute | solution.py:291
  299.6 64.3 %collective-permute-start.43 = (bf16[4,4,8,8,256]{4,3,2,1,0:T(8,128)(2,1)}, bf16[4,4,8,8,256]{4,3,2,1,0:T(8,128)(2,1)}, u32[]{:S(2)}, u32[]{:S(2)}) collective-permute-start(bf16[4,4,8,8,256]{4,3,2,1,0:T(8,128)(2,1)} %get-tuple-element.80), channel_id=1, source_target_pairs={{0,12},{1,13},{2,14},{3,15},{4,8},{5,9},{6,10},{7,11},{8,4},{9,5},... | collective-permute-start | bytes 1572872 | tf_op jit(solution)/shard_map/ppermute | solution.py:282
  315.4 49.8 %collective-permute-start.35 = (bf16[4,4,8,8,256]{4,3,2,1,0:T(8,128)(2,1)S(1)}, bf16[4,4,8,8,256]{4,3,2,1,0:T(8,128)(2,1)S(1)}, u32[]{:S(2)}, u32[]{:S(2)}) collective-permute-start(bf16[4,4,8,8,256]{4,3,2,1,0:T(8,128)(2,1)S(1)} %copy-done.25), channel_id=1, source_target_pairs={{0,4},{1,5},{2,6},{3,7},{4,0},{5,1},{6,2},{7,3},{8,12},{9,13},{10,... | collective-permute-start | bytes 1572872 | tf_op jit(solution)/shard_map/ppermute | solution.py:282
  324.8 59.2 %collective-permute-start.36 = (bf16[4,4,8,8,256]{4,3,2,1,0:T(8,128)(2,1)S(1)}, bf16[4,4,8,8,256]{4,3,2,1,0:T(8,128)(2,1)S(1)}, u32[]{:S(2)}, u32[]{:S(2)}) collective-permute-start(bf16[4,4,8,8,256]{4,3,2,1,0:T(8,128)(2,1)S(1)} %copy-done.23), channel_id=1, source_target_pairs={{0,8},{1,9},{2,10},{3,11},{4,12},{5,13},{6,14},{7,15},{8,0},{9,1},... | collective-permute-start | bytes 1572872 | tf_op jit(solution)/shard_map/ppermute | solution.py:282
  325.5 71.9 %collective-permute-start.37 = (bf16[4,4,8,8,256]{4,3,2,1,0:T(8,128)(2,1)S(1)}, bf16[4,4,8,8,256]{4,3,2,1,0:T(8,128)(2,1)S(1)}, u32[]{:S(2)}, u32[]{:S(2)}) collective-permute-start(bf16[4,4,8,8,256]{4,3,2,1,0:T(8,128)(2,1)S(1)} %copy-done.22), channel_id=1, source_target_pairs={{0,12},{1,13},{2,14},{3,15},{4,8},{5,9},{6,10},{7,11},{8,4},{9,5},... | collective-permute-start | bytes 1572872 | tf_op jit(solution)/shard_map/ppermute | solution.py:282
  363.9 34.4 %collective-permute-start.52 = (bf16[16,8,32,128]{3,2,1,0:T(8,128)(2,1)S(1)}, bf16[16,8,32,128]{3,2,1,0:T(8,128)(2,1)S(1)}, u32[]{:S(2)}, u32[]{:S(2)}) collective-permute-start(bf16[16,8,32,128]{3,2,1,0:T(8,128)(2,1)S(1)} %fusion), channel_id=1, source_target_pairs={{0,16},{16,0},{1,17},{17,1},{2,18},{18,2},{3,19},{19,3},{4,20},{20... | collective-permute-start | bytes 3145736 | tf_op jit(solution)/shard_map/ppermute | solution.py:291
  365.2 40.6 %collective-permute-start.50 = (bf16[2,2,16,8,512]{4,3,2,1,0:T(8,128)(2,1)S(1)}, bf16[2,2,16,8,512]{4,3,2,1,0:T(8,128)(2,1)S(1)}, u32[]{:S(2)}, u32[]{:S(2)}) collective-permute-start(bf16[2,2,16,8,512]{4,3,2,1,0:T(8,128)(2,1)S(1)} %add_convert_fusion), channel_id=1, source_target_pairs={{0,8},{1,9},{2,10},{3,11},{4,12},{5,13},{6,14},{7,15},{8,0},{9,1},... | collective-permute-start | bytes 1572872 | tf_op jit(solution)/shard_map/ppermute | solution.py:282
  405.8 42.4 %collective-permute-start.45 = (bf16[4,4,8,8,256]{4,3,2,1,0:T(8,128)(2,1)S(1)}, bf16[4,4,8,8,256]{4,3,2,1,0:T(8,128)(2,1)S(1)}, u32[]{:S(2)}, u32[]{:S(2)}) collective-permute-start(bf16[4,4,8,8,256]{4,3,2,1,0:T(8,128)(2,1)S(1)} %pad_maximum_fusion.13), channel_id=1, source_target_pairs={{0,2},{1,3},{2,0},{3,1},{4,6},{5,7},{6,4},{7,5},{8,10},{9,11},{10,... | collective-permute-start | bytes 1572872 | tf_op jit(solution)/shard_map/ppermute | solution.py:282
  406.8 41.4 %collective-permute-start.46 = (bf16[4,4,8,8,256]{4,3,2,1,0:T(8,128)(2,1)S(1)}, bf16[4,4,8,8,256]{4,3,2,1,0:T(8,128)(2,1)S(1)}, u32[]{:S(2)}, u32[]{:S(2)}) collective-permute-start(bf16[4,4,8,8,256]{4,3,2,1,0:T(8,128)(2,1)S(1)} %pad_maximum_fusion.14), channel_id=1, source_target_pairs={{0,3},{1,2},{2,1},{3,0},{4,7},{5,6},{6,5},{7,4},{8,11},{9,10},{10,... | collective-permute-start | bytes 1572872 | tf_op jit(solution)/shard_map/ppermute | solution.py:282
  408.2 40.1 %collective-permute-start.38 = (bf16[4,4,8,8,256]{4,3,2,1,0:T(8,128)(2,1)S(1)}, bf16[4,4,8,8,256]{4,3,2,1,0:T(8,128)(2,1)S(1)}, u32[]{:S(2)}, u32[]{:S(2)}) collective-permute-start(bf16[4,4,8,8,256]{4,3,2,1,0:T(8,128)(2,1)S(1)} %pad_maximum_fusion.9), channel_id=1, source_target_pairs={{0,1},{1,0},{2,3},{3,2},{4,5},{5,4},{6,7},{7,6},{8,9},{9,8},{10,11... | collective-permute-start | bytes 1572872 | tf_op jit(solution)/shard_map/ppermute | solution.py:282
  413.0 44.6 %collective-permute-start.39 = (bf16[4,4,8,8,256]{4,3,2,1,0:T(8,128)(2,1)S(1)}, bf16[4,4,8,8,256]{4,3,2,1,0:T(8,128)(2,1)S(1)}, u32[]{:S(2)}, u32[]{:S(2)}) collective-permute-start(bf16[4,4,8,8,256]{4,3,2,1,0:T(8,128)(2,1)S(1)} %pad_maximum_fusion.10), channel_id=1, source_target_pairs={{0,2},{1,3},{2,0},{3,1},{4,6},{5,7},{6,4},{7,5},{8,10},{9,11},{10,... | collective-permute-start | bytes 1572872 | tf_op jit(solution)/shard_map/ppermute | solution.py:282
  (81 other events, 1295.1 us)

commit v2 on v1

--- a/solution.py
+++ b/solution.py
@@ -15,7 +15,7 @@
 PAIR = 2
 
 GO = ("z", "xy")
-COME = ("z", "z")
+COME = ("z", "xy")
 
 
 def gelu_tanh(value):
@@ -154,8 +154,8 @@
 
 def middle_kernel(go, come, who, *refs):
     x_near, x_far, tb, w_ref = refs[:4], refs[4:7], refs[7], refs[8]
-    fb_out, ta_out, g_ref = refs[9:13], refs[13:21], refs[21]
-    sg, tg = refs[22], refs[23]
+    fb_out, ta_out, g_ref = refs[9:13], refs[13], refs[14]
+    sg, tg = refs[15], refs[16]
     f = who[0]
 
     def place(s, first):
@@ -185,7 +185,7 @@
             0.7978845608028654 + (3 * 0.7978845608028654 * 0.044715) * vv
         )
         pre_grad = (hidden_grad * slope).astype(BF)
-        ta_out[q][:, 0] = dot(w3t, hidden).reshape(16, 8, TT).astype(BF)
+        ta_out[at, :, 0] = dot(w3t, hidden).reshape(16, 8, TT).astype(BF)
         fb = dot(w2, pre_grad)
         for s in range(16):
             i, j = place(s, come)
@@ -205,11 +205,11 @@
 
 
 def token_kernel(who, *refs):
-    pieces, og, a_ref, out, g_ref = refs[:16], refs[16], refs[17], refs[18], refs[19]
+    pieces, og, a_ref, out, g_ref = refs[:2], refs[2], refs[3], refs[4], refs[5]
     f, tok = who[0], who[1]
     for n in range(STEP):
         at = (f & (STEP - 1)) ^ n
-        parts = [piece[at] for piece in pieces]
+        parts = [pieces[r >> 3][(f & 7) ^ (r & 7), at] for r in range(16)]
         rows = jnp.concatenate([part.astype(F32).reshape(32, TT) for part in parts], axis=0).astype(BF)
         out[group_rows(at), :] = dot(gathered(who, a_ref, n), rows, 0, 0).astype(BF)
         g = compacted(dot(rows, og[group_rows(at), :], 1, 1))
@@ -348,7 +348,6 @@
     results = {}
     near_spec = pl.BlockSpec((1, 1, tiles, 8, TT), lambda l, w: (0, l, 0, 0, 0))
     far_spec = pl.BlockSpec((4, 1, tiles, 8, TT), lambda l, w: (0, l, 0, 0, 0))
-    act_spec = pl.BlockSpec((16, 1, 8, TT), lambda l, w: (0, l, 0, 0))
     rows_spec = pl.BlockSpec((8, 16, 1, 8, TT), lambda l, w: (0, 0, l, 0, 0))
     for h in order:
         w_spec = pl.BlockSpec((1, 2, 16, 8, hidden), lambda l, w, h=h: (l ^ (2 * w[1] * h), 0, 0, 0, 0))
@@ -356,13 +355,13 @@
         results[h] = call(
             functools.partial(middle_kernel, GO[h], COME[h]), (4,),
             [near_spec] * 4 + [far_spec] * 3 + [rows_spec, w_spec],
-            [far_spec] * 4 + [act_spec] * 8 + [g_spec],
-            [group] * 4 + [shape((16, 4, 8, TT))] * 8 + [shape((4, 2, 16, 8, hidden), F32)],
+            [far_spec] * 4 + [rows_spec, g_spec],
+            [group] * 4 + [shape((8, 16, 4, 8, TT))] + [shape((4, 2, 16, 8, hidden), F32)],
             [pltpu.VMEM((128, hidden), F32)] * 2,
             12 * 4 * 128 * hidden * tok_dev // 2, 20 * 2**20,
         )(who, *arrived[h], back[h], w_far if h else w_own)
     returned = {h: two_stage(results[h][:4], COME[h]) for h in order}
-    acts = {h: [results[h][4]] + [flip(results[h][4 + s], s) for s in range(1, 8)] for h in order}
+    acts = {h: spread(results[h][4]) for h in order}
 
     near_spec = pl.BlockSpec((1, 4, PAIR, 8, TT), lambda e, t, w: (0, 0, t, 0, 0))
     far_spec = pl.BlockSpec((4, 4, PAIR, 8, TT), lambda e, t, w: (0, 0, t, 0, 0))
@@ -379,18 +378,18 @@
 
     layer_out, fourth = call(
         token_kernel, (16 // STEP,),
-        [pl.BlockSpec((STEP, 4, 8, TT), lambda n, w: ((w[0] // STEP) ^ n, 0, 0, 0))] * 16 + [og_spec, a_spec],
+        [pl.BlockSpec((8, STEP, 4, 8, TT), lambda n, w: (0, (w[0] // STEP) ^ n, 0, 0, 0))] * 2 + [og_spec, a_spec],
         [og_spec, a_spec],
         [shape((8192, tok_part)), shape((2, 16, 8, 32, width), F32)], (),
         4 * 512 * 8192 * TT, 6 * 8192 * TT,
-    )(who, *acts[0], *acts[1], output_grad, a_all)
+    )(who, acts[0], acts[1], output_grad, a_all)
 
     def both(mine):
         other = swap(mine)
         low, high = jnp.where(tok == 0, mine, other), jnp.where(tok == 0, other, mine)
         return jnp.concatenate([low, high], axis=0)
 
-    kept = [results[h][12][:2] + swap(results[h][12][2:].astype(BF)).astype(F32) for h in (0, 1)]
+    kept = [results[h][5][:2] + swap(results[h][5][2:].astype(BF)).astype(F32) for h in (0, 1)]
     middle = both(kept[0] + flip(kept[1].astype(BF), 8).astype(F32)) * scale
     second = middle[:, 0].reshape(CB, 16, 2, CB, hidden).transpose(0, 2, 1, 3, 4).reshape(CB, width, hidden)
     third = middle[:, 1].reshape(CB, 16, 2, CB, hidden).transpose(0, 4, 2, 1, 3).reshape(CB, hidden, width)

time: 485 us -> 509 us (1.049)
  blocking collectives: 0 us -> 30 us
  starting transfers between devices: 88.5 us -> 80.1 us
  other arithmetic: 6.7 us -> 15.1 us
  waiting for transfers between devices: 267 us -> 260 us
    all_to_all x0 -> x1, blocking collectives: none -> 30 us  [spread(): lax.all_to_all(value, 'feat', 0, 0, axis_index_groups=groups, tiled=True)]
    ppermute x52 -> x38, starting transfers between devices: 76.7 us -> 54.1 us  [flip(): return lax.ppermute(value, 'feat', [(i, i ^ bits) for i in range(16)])]
    all_to_all x2 -> x3, waiting for transfers between devices: 17.7 us -> 0.01 us  [spread(): lax.all_to_all(value, 'feat', 0, 0, axis_index_groups=groups, tiled=True)]
    all_to_all x2 -> x3, starting transfers between devices: 11 us -> 25.5 us  [spread(): lax.all_to_all(value, 'feat', 0, 0, axis_index_groups=groups, tiled=True)]
    ppermute x52 -> x38, waiting for transfers between devices: 247 us -> 258 us  [flip(): return lax.ppermute(value, 'feat', [(i, i ^ bits) for i in range(16)])]
    another operation x12, other arithmetic: 0.83 us -> 6.49 us  [two_stage(): far = [flip(jnp.stack([n[j] for n in near]), two * j) for j in (1, 2, 3)]]
    unnamed x107 -> x59, local copies, waits for them, and re-layouts: 12.4 us -> 8.94 us
  transfers between devices with their start and end apart: 62 -> 49, of which waited for: 29 -> 26; matrix products, arithmetic and copies ran while one was open for 4% -> 7% of each run, Pallas kernels for 17% -> 16%
where the time goes in v2:
time: 509 us; the launch traced here: 504 us
  waiting for transfers between devices  260 us (51%)
  Pallas kernels  89.4 us (18%)
  starting transfers between devices  80.1 us (16%)
  blocking collectives  30 us (6%)
  local copies, waits for them, and re-layouts  28.1 us (6%)
  other arithmetic  15.1 us (3%)
    ppermute x38, waiting for transfers between devices, flip(): return lax.ppermute(value, 'feat', [(i, i ^ bits) for i in range(16)])  258 us
    ppermute x38, starting transfers between devices, flip(): return lax.ppermute(value, 'feat', [(i, i ^ bits) for i in range(16)])  54.1 us
    pallas_call x2, Pallas kernels, local_halves(): call(functools.partial(middle_kernel, GO[h], COME[h]), (4,), [near_spec]...  52.1 us
    all_to_all x1, blocking collectives, spread(): lax.all_to_all(value, 'feat', 0, 0, axis_index_groups=groups, tiled=True)  30 us
    all_to_all x3, starting transfers between devices, spread(): lax.all_to_all(value, 'feat', 0, 0, axis_index_groups=groups, tiled=True)  25.5 us
    pallas_call x1, Pallas kernels, local_halves(): call(functools.partial(finish_kernel, COME), (2, steps), ([near_spec] * 4...  12.4 us
    pallas_call x1, Pallas kernels, local_halves(): call(token_kernel, (16 // STEP,), [pl.BlockSpec((8, STEP, 4, 8, TT), lamb...  10.7 us
  transfers between devices with their start and end apart: 49, of which 26 were waited for; matrix products, arithmetic and copies ran while one was open for 7% of the time, Pallas kernels for 16%

profile of v2, /device:TPU:14, one launch (start us, length us, event | category | flops | bytes accessed | tf_op | source)
XLA Modules:
  0.0 504.0 jit_solution(7809403971539684304)
XLA Ops:
  5.8 3.1 collective-permute-done.8
  14.1 4.8 collective-permute-done.10
  20.2 4.1 collective-permute-done.11
  28.7 7.3 %shard_map.110 = (bf16[8,16,4,8,256]{4,3,2,1,0:T(8,128)(2,1)}, bf16[8,16,4,8,256]{4,3,2,1,0:T(8,128)(2,1)}) custom-call(s32[3]{0:T(128)} %pad_add_fusion.who, bf16[8192,256]{1,0:T(8,128)(2,1)} %refs_2_.1, bf16[2,16,8,32,128]{4,3,2,1,0:T(8,128)(2,1)} %pad_maximum_fusion.a_ref.refs_3_), custom_call_target="tpu_custom_call" | custom-call | flops 2147483648 | bytes 8388608 | tf_op jit(solution)/shard_map/pallas_call | solution.py:341
  35.9 30.0 %all_to_all.20.refs_7_ = bf16[8,16,4,8,256]{4,3,2,1,0:T(8,128)(2,1)} all-to-all(bf16[8,16,4,8,256]{4,3,2,1,0:T(8,128)(2,1)} %get-tuple-element.36), channel_id=1, replica_groups={{0,1,2,3,4,5,6,7},{8,9,10,11,12,13,14,15},{16,17,18,19,20,21,22,23},{24..., dimensions={0} | all-to-all | bytes 4194304 | tf_op jit(solution)/shard_map/all_to_all | solution.py:287
  66.0 6.6 %all-to-all-start.2 = ((bf16[8,16,4,8,256]{4,3,2,1,0:T(8,128)(2,1)}), bf16[8,16,4,8,256]{4,3,2,1,0:T(8,128)(2,1)S(1)}, u32[]{:S(2)}, u32[]{:S(2)}) async-start(bf16[8,16,4,8,256]{4,3,2,1,0:T(8,128)(2,1)} %get-tuple-element.42), calls=%async_computation.2 | async-start | bytes 4194304 | tf_op jit(solution)/shard_map/all_to_all | solution.py:287
  73.5 7.0 %shard_map.109 = (bf16[4,4,8,8,256]{4,3,2,1,0:T(8,128)(2,1)}, bf16[4,4,8,8,256]{4,3,2,1,0:T(8,128)(2,1)}, bf16[4,4,8,8,256]{4,3,2,1,0:T(8,128)(2,1)}, bf16[4,4,8...) custom-call(s32[3]{0:T(128)} %pad_add_fusion.who, ...), custom_call_target="tpu_custom_call" | custom-call | flops 2147483648 | bytes 8388608 | tf_op jit(solution)/shard_map/pallas_call | solution.py:329
  85.0 44.3 %collective-permute-done.refs_1_ = bf16[4,4,8,8,256]{4,3,2,1,0:T(8,128)(2,1)S(1)} collective-permute-done((bf16[4,4,8,8,256]{4,3,2,1,0:T(8,128)(2,1)}, bf16[4,4,8,8,256]{4,3,2,1,0:T(8,128)(2,1)S(1)}, u32[]{:S(2)}, u32[]{:S(2)}) %collective-permute-start) | collective-permute-done | bytes 524320 | tf_op jit(solution)/shard_map/ppermute | solution.py:282
  140.5 6.5 %collective-permute-done.4.refs_5_ = bf16[4,4,8,8,256]{4,3,2,1,0:T(8,128)(2,1)} collective-permute-done((bf16[4,4,8,8,256]{4,3,2,1,0:T(8,128)(2,1)}, bf16[4,4,8,8,256]{4,3,2,1,0:T(8,128)(2,1)}, u32[]{:S(2)}, u32[]{:S(2)}) %collective-permute-start.4) | collective-permute-done | bytes 524320 | tf_op jit(solution)/shard_map/ppermute | solution.py:282
  147.0 26.0 %shard_map.111 = (bf16[4,4,8,8,256]{4,3,2,1,0:T(8,128)(2,1)}, bf16[4,4,8,8,256]{4,3,2,1,0:T(8,128)(2,1)}, bf16[4,4,8,8,256]{4,3,2,1,0:T(8,128)(2,1)}, bf16[4,4,8...) custom-call(s32[3]{0:T(128)} %pad_add_fusion.who, ...), custom_call_target="tpu_custom_call" | custom-call | flops 6442450944 | bytes 20971520 | tf_op jit(solution)/shard_map/pallas_call | solution.py:355
  174.5 13.6 %all-to-all-start.1 = ((bf16[8,16,4,8,256]{4,3,2,1,0:T(8,128)(2,1)}), bf16[8,16,4,8,256]{4,3,2,1,0:T(8,128)(2,1)S(1)}, u32[]{:S(2)}, u32[]{:S(2)}) async-start(bf16[8,16,4,8,256]{4,3,2,1,0:T(8,128)(2,1)} %get-tuple-element.37), calls=%async_computation.1 | async-start | bytes 4194304 | tf_op jit(solution)/shard_map/all_to_all | solution.py:287
  195.5 25.1 %collective-permute-done.13.refs_1_ = bf16[4,4,8,8,256]{4,3,2,1,0:T(8,128)(2,1)} collective-permute-done((bf16[4,4,8,8,256]{4,3,2,1,0:T(8,128)(2,1)}, bf16[4,4,8,8,256]{4,3,2,1,0:T(8,128)(2,1)}, u32[]{:S(2)}, u32[]{:S(2)}) %collective-permute-start.13) | collective-permute-done | bytes 524320 | tf_op jit(solution)/shard_map/ppermute | solution.py:282
  222.7 6.9 %collective-permute-done.15.refs_3_ = bf16[4,4,8,8,256]{4,3,2,1,0:T(8,128)(2,1)S(1)} collective-permute-done((bf16[4,4,8,8,256]{4,3,2,1,0:T(8,128)(2,1)}, bf16[4,4,8,8,256]{4,3,2,1,0:T(8,128)(2,1)S(1)}, u32[]{:S(2)}, u32[]{:S(2)}) %collective-permute-start.15) | collective-permute-done | bytes 524320 | tf_op jit(solution)/shard_map/ppermute | solution.py:282
  230.5 4.5 collective-permute-start.17
  236.2 12.5 %collective-permute-done.16.refs_4_ = bf16[4,4,8,8,256]{4,3,2,1,0:T(8,128)(2,1)S(1)} collective-permute-done((bf16[4,4,8,8,256]{4,3,2,1,0:T(8,128)(2,1)S(1)}, bf16[4,4,8,8,256]{4,3,2,1,0:T(8,128)(2,1)S(1)}, u32[]{:S(2)}, u32[]{:S(2)}) %collective-permute-start.16) | collective-permute-done | bytes 524320 | tf_op jit(solution)/shard_map/ppermute | solution.py:282
  248.6 21.2 %collective-permute-done.17.refs_5_ = bf16[4,4,8,8,256]{4,3,2,1,0:T(8,128)(2,1)S(1)} collective-permute-done((bf16[4,4,8,8,256]{4,3,2,1,0:T(8,128)(2,1)S(1)}, bf16[4,4,8,8,256]{4,3,2,1,0:T(8,128)(2,1)S(1)}, u32[]{:S(2)}, u32[]{:S(2)}) %collective-permute-start.17) | collective-permute-done | bytes 524320 | tf_op jit(solution)/shard_map/ppermute | solution.py:282
  269.8 10.8 %collective-permute-done.18.refs_6_ = bf16[4,4,8,8,256]{4,3,2,1,0:T(8,128)(2,1)S(1)} collective-permute-done((bf16[4,4,8,8,256]{4,3,2,1,0:T(8,128)(2,1)S(1)}, bf16[4,4,8,8,256]{4,3,2,1,0:T(8,128)(2,1)S(1)}, u32[]{:S(2)}, u32[]{:S(2)}) %collective-permute-start.18) | collective-permute-done | bytes 524320 | tf_op jit(solution)/shard_map/ppermute | solution.py:282
  281.4 26.1 %shard_map.112 = (bf16[4,4,8,8,256]{4,3,2,1,0:T(8,128)(2,1)}, bf16[4,4,8,8,256]{4,3,2,1,0:T(8,128)(2,1)}, bf16[4,4,8,8,256]{4,3,2,1,0:T(8,128)(2,1)}, bf16[4,4,8...) custom-call(s32[3]{0:T(128)} %pad_add_fusion.who, ...), custom_call_target="tpu_custom_call" | custom-call | flops 6442450944 | bytes 20971520 | tf_op jit(solution)/shard_map/pallas_call | solution.py:355
  308.8 5.3 %all-to-all-start.3 = ((bf16[8,16,4,8,256]{4,3,2,1,0:T(8,128)(2,1)}), bf16[8,16,4,8,256]{4,3,2,1,0:T(8,128)(2,1)}, u32[]{:S(2)}, u32[]{:S(2)}) async-start(bf16[8,16,4,8,256]{4,3,2,1,0:T(8,128)(2,1)} %get-tuple-element.43), calls=%async_computation.3 | async-start | bytes 4194304 | tf_op jit(solution)/shard_map/all_to_all | solution.py:287
  322.0 28.8 %collective-permute-done.27.refs_8_ = bf16[4,4,8,8,256]{4,3,2,1,0:T(8,128)(2,1)S(1)} collective-permute-done((bf16[4,4,8,8,256]{4,3,2,1,0:T(8,128)(2,1)}, bf16[4,4,8,8,256]{4,3,2,1,0:T(8,128)(2,1)S(1)}, u32[]{:S(2)}, u32[]{:S(2)}) %collective-permute-start.27) | collective-permute-done | bytes 524320 | tf_op jit(solution)/shard_map/ppermute | solution.py:282
  350.8 4.4 collective-permute-start.22
  355.3 6.3 %collective-permute-done.29.refs_10_ = bf16[4,4,8,8,256]{4,3,2,1,0:T(8,128)(2,1)S(1)} collective-permute-done((bf16[4,4,8,8,256]{4,3,2,1,0:T(8,128)(2,1)}, bf16[4,4,8,8,256]{4,3,2,1,0:T(8,128)(2,1)S(1)}, u32[]{:S(2)}, u32[]{:S(2)}) %collective-permute-start.29) | collective-permute-done | bytes 524320 | tf_op jit(solution)/shard_map/ppermute | solution.py:282
  364.1 4.7 collective-permute-start.31
  368.8 21.8 %collective-permute-done.22.refs_2_ = bf16[4,4,8,8,256]{4,3,2,1,0:T(8,128)(2,1)S(1)} collective-permute-done((bf16[4,4,8,8,256]{4,3,2,1,0:T(8,128)(2,1)S(1)}, bf16[4,4,8,8,256]{4,3,2,1,0:T(8,128)(2,1)S(1)}, u32[]{:S(2)}, u32[]{:S(2)}) %collective-permute-start.22) | collective-permute-done | bytes 524320 | tf_op jit(solution)/shard_map/ppermute | solution.py:282
  390.7 32.8 %collective-permute-done.23.refs_3_ = bf16[4,4,8,8,256]{4,3,2,1,0:T(8,128)(2,1)S(1)} collective-permute-done((bf16[4,4,8,8,256]{4,3,2,1,0:T(8,128)(2,1)S(1)}, bf16[4,4,8,8,256]{4,3,2,1,0:T(8,128)(2,1)S(1)}, u32[]{:S(2)}, u32[]{:S(2)}) %collective-permute-start.23) | collective-permute-done | bytes 524320 | tf_op jit(solution)/shard_map/ppermute | solution.py:282
  430.6 10.7 %shard_map.113 = (bf16[8192,256]{1,0:T(8,128)(2,1)}, f32[2,16,8,32,128]{4,3,2,1,0:T(8,128)}) custom-call(s32[3]{0:T(128)} %pad_add_fusion.who, bf16[8,16,4,8,256]{4,3,2,1,0:T(8,128)(2,1)} %copy-done, bf16[8,16,4,8,256]{4,3,2,1,0:T(8,128)(2,1)} %all-to-all-done.3.refs_1_, bf16[8192,256]{1,0:T(8,128)(2,1)} %refs_2_.1, ...), custom_call_target="tpu_custom_call" | custom-call | flops 4294967296 | bytes 12582912 | tf_op jit(solution)/shard_map/pallas_call | solution.py:379
  448.9 12.4 %shard_map.114 = (bf16[512,4096]{1,0:T(8,128)(2,1)}, f32[16,32,128]{2,1,0:T(8,128)}) custom-call(s32[3]{0:T(128)} %pad_add_fusion.who, bf16[4,4,8,8,256]{4,3,2,1,0:T(8,128)(2,1)} %get-tuple-element.45.refs_0_, bf16[4,4,8,8,256]{4,3,2,1,0:T(8,128)(2,1)} %copy-done.11, bf16[4,4,8,8,256]{4,3,2,1,0:T(8,128)(2,1)} %copy-done.12, ...), custom_call_target="tpu_custom_call" | custom-call | flops 4294967296 | bytes 12582912 | tf_op jit(solution)/shard_map/pallas_call | solution.py:370
  461.5 5.7 %collective-permute-done.36 = bf16[2,2,16,8,512]{4,3,2,1,0:T(8,128)(2,1)S(1)} collective-permute-done((bf16[2,2,16,8,512]{4,3,2,1,0:T(8,128)(2,1)S(1)}, bf16[2,2,16,8,512]{4,3,2,1,0:T(8,128)(2,1)S(1)}, u32[]{:S(2)}, u32[]{:S(2)}) %collective-permute-start.36) | collective-permute-done | bytes 524320 | tf_op jit(solution)/shard_map/ppermute | solution.py:282
  475.6 5.4 %collective-permute-done.39 = bf16[4,8,32,128]{3,2,1,0:T(8,128)(2,1)S(1)} collective-permute-done((bf16[4,8,32,128]{3,2,1,0:T(8,128)(2,1)S(1)}, bf16[4,8,32,128]{3,2,1,0:T(8,128)(2,1)S(1)}, u32[]{:S(2)}, u32[]{:S(2)}) %collective-permute-start.39) | collective-permute-done | bytes 262176 | tf_op jit(solution)/shard_map/ppermute | solution.py:282
  481.1 5.3 %collective-permute-done.41 = bf16[4,8,32,128]{3,2,1,0:T(8,128)(2,1)S(1)} collective-permute-done((bf16[4,8,32,128]{3,2,1,0:T(8,128)(2,1)S(1)}, bf16[4,8,32,128]{3,2,1,0:T(8,128)(2,1)S(1)}, u32[]{:S(2)}, u32[]{:S(2)}) %collective-permute-start.41) | collective-permute-done | bytes 262176 | tf_op jit(solution)/shard_map/ppermute | solution.py:282
  488.0 4.5 collective-permute-start.42
  495.2 3.5 collective-permute-done.44
  (198 shorter events, 91.0 us)
Async XLA Ops:
  66.0 107.1 %all-to-all-start.2 = ((bf16[8,16,4,8,256]{4,3,2,1,0:T(8,128)(2,1)}), bf16[8,16,4,8,256]{4,3,2,1,0:T(8,128)(2,1)S(1)}, u32[]{:S(2)}, u32[]{:S(2)}) async-start(bf16[8,16,4,8,256]{4,3,2,1,0:T(8,128)(2,1)} %get-tuple-element.42), calls=%async_computation.2 | async-start | bytes 4194304 | tf_op jit(solution)/shard_map/all_to_all | solution.py:287
  80.4 48.9 %collective-permute-start = (bf16[4,4,8,8,256]{4,3,2,1,0:T(8,128)(2,1)}, bf16[4,4,8,8,256]{4,3,2,1,0:T(8,128)(2,1)S(1)}, u32[]{:S(2)}, u32[]{:S(2)}) collective-permute-start(bf16[4,4,8,8,256]{4,3,2,1,0:T(8,128)(2,1)} %get-tuple-element.33), channel_id=1, source_target_pairs={{0,4},{1,5},{2,6},{3,7},{4,0},{5,1},{6,2},{7,3},{8,12},{9,13},{10,... | collective-permute-start | bytes 1572872 | tf_op jit(solution)/shard_map/ppermute | solution.py:282
  81.0 49.1 %collective-permute-start.1 = (bf16[4,4,8,8,256]{4,3,2,1,0:T(8,128)(2,1)}, bf16[4,4,8,8,256]{4,3,2,1,0:T(8,128)(2,1)S(1)}, u32[]{:S(2)}, u32[]{:S(2)}) collective-permute-start(bf16[4,4,8,8,256]{4,3,2,1,0:T(8,128)(2,1)} %get-tuple-element.34), channel_id=1, source_target_pairs={{0,8},{1,9},{2,10},{3,11},{4,12},{5,13},{6,14},{7,15},{8,0},{9,1},... | collective-permute-start | bytes 1572872 | tf_op jit(solution)/shard_map/ppermute | solution.py:282
  81.8 48.3 %collective-permute-start.2 = (bf16[4,4,8,8,256]{4,3,2,1,0:T(8,128)(2,1)}, bf16[4,4,8,8,256]{4,3,2,1,0:T(8,128)(2,1)S(1)}, u32[]{:S(2)}, u32[]{:S(2)}) collective-permute-start(bf16[4,4,8,8,256]{4,3,2,1,0:T(8,128)(2,1)} %get-tuple-element.35), channel_id=1, source_target_pairs={{0,12},{1,13},{2,14},{3,15},{4,8},{5,9},{6,10},{7,11},{8,4},{9,5},... | collective-permute-start | bytes 1572872 | tf_op jit(solution)/shard_map/ppermute | solution.py:282
  131.9 15.1 %collective-permute-start.4 = (bf16[4,4,8,8,256]{4,3,2,1,0:T(8,128)(2,1)}, bf16[4,4,8,8,256]{4,3,2,1,0:T(8,128)(2,1)}, u32[]{:S(2)}, u32[]{:S(2)}) collective-permute-start(bf16[4,4,8,8,256]{4,3,2,1,0:T(8,128)(2,1)} %pad_maximum_fusion.4), channel_id=1, source_target_pairs={{0,2},{1,3},{2,0},{3,1},{4,6},{5,7},{6,4},{7,5},{8,10},{9,11},{10,... | collective-permute-start | bytes 1572872 | tf_op jit(solution)/shard_map/ppermute | solution.py:282
  174.5 133.0 %all-to-all-start.1 = ((bf16[8,16,4,8,256]{4,3,2,1,0:T(8,128)(2,1)}), bf16[8,16,4,8,256]{4,3,2,1,0:T(8,128)(2,1)S(1)}, u32[]{:S(2)}, u32[]{:S(2)}) async-start(bf16[8,16,4,8,256]{4,3,2,1,0:T(8,128)(2,1)} %get-tuple-element.37), calls=%async_computation.1 | async-start | bytes 4194304 | tf_op jit(solution)/shard_map/all_to_all | solution.py:287
  188.1 32.5 %collective-permute-start.13 = (bf16[4,4,8,8,256]{4,3,2,1,0:T(8,128)(2,1)}, bf16[4,4,8,8,256]{4,3,2,1,0:T(8,128)(2,1)}, u32[]{:S(2)}, u32[]{:S(2)}) collective-permute-start(bf16[4,4,8,8,256]{4,3,2,1,0:T(8,128)(2,1)} %get-tuple-element.39), channel_id=1, source_target_pairs={{0,1},{1,0},{2,3},{3,2},{4,5},{5,4},{6,7},{7,6},{8,9},{9,8},{10,11... | collective-permute-start | bytes 1572872 | tf_op jit(solution)/shard_map/ppermute | solution.py:282
  188.6 33.0 %collective-permute-start.14 = (bf16[4,4,8,8,256]{4,3,2,1,0:T(8,128)(2,1)}, bf16[4,4,8,8,256]{4,3,2,1,0:T(8,128)(2,1)}, u32[]{:S(2)}, u32[]{:S(2)}) collective-permute-start(bf16[4,4,8,8,256]{4,3,2,1,0:T(8,128)(2,1)} %get-tuple-element.40), channel_id=1, source_target_pairs={{0,2},{1,3},{2,0},{3,1},{4,6},{5,7},{6,4},{7,5},{8,10},{9,11},{10,... | collective-permute-start | bytes 1572872 | tf_op jit(solution)/shard_map/ppermute | solution.py:282
  189.2 41.2 %collective-permute-start.19 = (bf16[2,2,16,8,512]{4,3,2,1,0:T(8,128)(2,1)S(1)}, bf16[2,2,16,8,512]{4,3,2,1,0:T(8,128)(2,1)S(1)}, u32[]{:S(2)}, u32[]{:S(2)}) collective-permute-start(bf16[2,2,16,8,512]{4,3,2,1,0:T(8,128)(2,1)S(1)} %constant_dynamic-slice_fusion), channel_id=1, source_target_pairs={{0,8},{1,9},{2,10},{3,11},{4,12},{5,13},{6,14},{7,15},{8,0},{9,1},... | collective-permute-start | bytes 1572872 | tf_op jit(solution)/shard_map/ppermute | solution.py:282
  192.0 37.6 %collective-permute-start.15 = (bf16[4,4,8,8,256]{4,3,2,1,0:T(8,128)(2,1)}, bf16[4,4,8,8,256]{4,3,2,1,0:T(8,128)(2,1)S(1)}, u32[]{:S(2)}, u32[]{:S(2)}) collective-permute-start(bf16[4,4,8,8,256]{4,3,2,1,0:T(8,128)(2,1)} %get-tuple-element.41), channel_id=1, source_target_pairs={{0,3},{1,2},{2,1},{3,0},{4,7},{5,6},{6,5},{7,4},{8,11},{9,10},{10,... | collective-permute-start | bytes 1572872 | tf_op jit(solution)/shard_map/ppermute | solution.py:282
  229.7 18.9 %collective-permute-start.16 = (bf16[4,4,8,8,256]{4,3,2,1,0:T(8,128)(2,1)S(1)}, bf16[4,4,8,8,256]{4,3,2,1,0:T(8,128)(2,1)S(1)}, u32[]{:S(2)}, u32[]{:S(2)}) collective-permute-start(bf16[4,4,8,8,256]{4,3,2,1,0:T(8,128)(2,1)S(1)} %pad_maximum_fusion.6), channel_id=1, source_target_pairs={{0,4},{1,5},{2,6},{3,7},{4,0},{5,1},{6,2},{7,3},{8,12},{9,13},{10,... | collective-permute-start | bytes 1572872 | tf_op jit(solution)/shard_map/ppermute | solution.py:282
  230.5 39.3 %collective-permute-start.17 = (bf16[4,4,8,8,256]{4,3,2,1,0:T(8,128)(2,1)S(1)}, bf16[4,4,8,8,256]{4,3,2,1,0:T(8,128)(2,1)S(1)}, u32[]{:S(2)}, u32[]{:S(2)}) collective-permute-start(bf16[4,4,8,8,256]{4,3,2,1,0:T(8,128)(2,1)S(1)} %pad_maximum_fusion.7), channel_id=1, source_target_pairs={{0,8},{1,9},{2,10},{3,11},{4,12},{5,13},{6,14},{7,15},{8,0},{9,1},... | collective-permute-start | bytes 1572872 | tf_op jit(solution)/shard_map/ppermute | solution.py:282
  235.0 45.6 %collective-permute-start.18 = (bf16[4,4,8,8,256]{4,3,2,1,0:T(8,128)(2,1)S(1)}, bf16[4,4,8,8,256]{4,3,2,1,0:T(8,128)(2,1)S(1)}, u32[]{:S(2)}, u32[]{:S(2)}) collective-permute-start(bf16[4,4,8,8,256]{4,3,2,1,0:T(8,128)(2,1)S(1)} %pad_maximum_fusion.8), channel_id=1, source_target_pairs={{0,12},{1,13},{2,14},{3,15},{4,8},{5,9},{6,10},{7,11},{8,4},{9,5},... | collective-permute-start | bytes 1572872 | tf_op jit(solution)/shard_map/ppermute | solution.py:282
  308.8 121.9 %all-to-all-start.3 = ((bf16[8,16,4,8,256]{4,3,2,1,0:T(8,128)(2,1)}), bf16[8,16,4,8,256]{4,3,2,1,0:T(8,128)(2,1)}, u32[]{:S(2)}, u32[]{:S(2)}) async-start(bf16[8,16,4,8,256]{4,3,2,1,0:T(8,128)(2,1)} %get-tuple-element.43), calls=%async_computation.3 | async-start | bytes 4194304 | tf_op jit(solution)/shard_map/all_to_all | solution.py:287
  314.1 36.7 %collective-permute-start.27 = (bf16[4,4,8,8,256]{4,3,2,1,0:T(8,128)(2,1)}, bf16[4,4,8,8,256]{4,3,2,1,0:T(8,128)(2,1)S(1)}, u32[]{:S(2)}, u32[]{:S(2)}) collective-permute-start(bf16[4,4,8,8,256]{4,3,2,1,0:T(8,128)(2,1)} %get-tuple-element.50), channel_id=1, source_target_pairs={{0,1},{1,0},{2,3},{3,2},{4,5},{5,4},{6,7},{7,6},{8,9},{9,8},{10,11... | collective-permute-start | bytes 1572872 | tf_op jit(solution)/shard_map/ppermute | solution.py:282
  314.7 40.5 %collective-permute-start.28 = (bf16[4,4,8,8,256]{4,3,2,1,0:T(8,128)(2,1)}, bf16[4,4,8,8,256]{4,3,2,1,0:T(8,128)(2,1)S(1)}, u32[]{:S(2)}, u32[]{:S(2)}) collective-permute-start(bf16[4,4,8,8,256]{4,3,2,1,0:T(8,128)(2,1)} %get-tuple-element.51), channel_id=1, source_target_pairs={{0,2},{1,3},{2,0},{3,1},{4,6},{5,7},{6,4},{7,5},{8,10},{9,11},{10,... | collective-permute-start | bytes 1572872 | tf_op jit(solution)/shard_map/ppermute | solution.py:282
  317.0 44.6 %collective-permute-start.29 = (bf16[4,4,8,8,256]{4,3,2,1,0:T(8,128)(2,1)}, bf16[4,4,8,8,256]{4,3,2,1,0:T(8,128)(2,1)S(1)}, u32[]{:S(2)}, u32[]{:S(2)}) collective-permute-start(bf16[4,4,8,8,256]{4,3,2,1,0:T(8,128)(2,1)} %get-tuple-element.52), channel_id=1, source_target_pairs={{0,3},{1,2},{2,1},{3,0},{4,7},{5,6},{6,5},{7,4},{8,11},{9,10},{10,... | collective-permute-start | bytes 1572872 | tf_op jit(solution)/shard_map/ppermute | solution.py:282
  321.3 104.0 %collective-permute-start.35 = (bf16[2,2,16,8,512]{4,3,2,1,0:T(8,128)(2,1)S(1)}, bf16[2,2,16,8,512]{4,3,2,1,0:T(8,128)(2,1)S(1)}, u32[]{:S(2)}, u32[]{:S(2)}) collective-permute-start(bf16[2,2,16,8,512]{4,3,2,1,0:T(8,128)(2,1)S(1)} %slice.334), channel_id=1, source_target_pairs={{0,16},{16,0},{1,17},{17,1},{2,18},{18,2},{3,19},{19,3},{4,20},{20... | collective-permute-start | bytes 1572872 | tf_op jit(solution)/shard_map/ppermute | solution.py:291
  321.3 42.7 %collective-permute-start.21 = (bf16[4,4,8,8,256]{4,3,2,1,0:T(8,128)(2,1)S(1)}, bf16[4,4,8,8,256]{4,3,2,1,0:T(8,128)(2,1)S(1)}, u32[]{:S(2)}, u32[]{:S(2)}) collective-permute-start(bf16[4,4,8,8,256]{4,3,2,1,0:T(8,128)(2,1)S(1)} %copy-done.22), channel_id=1, source_target_pairs={{0,4},{1,5},{2,6},{3,7},{4,0},{5,1},{6,2},{7,3},{8,12},{9,13},{10,... | collective-permute-start | bytes 1572872 | tf_op jit(solution)/shard_map/ppermute | solution.py:282
  350.8 39.9 %collective-permute-start.22 = (bf16[4,4,8,8,256]{4,3,2,1,0:T(8,128)(2,1)S(1)}, bf16[4,4,8,8,256]{4,3,2,1,0:T(8,128)(2,1)S(1)}, u32[]{:S(2)}, u32[]{:S(2)}) collective-permute-start(bf16[4,4,8,8,256]{4,3,2,1,0:T(8,128)(2,1)S(1)} %copy-done.21), channel_id=1, source_target_pairs={{0,8},{1,9},{2,10},{3,11},{4,12},{5,13},{6,14},{7,15},{8,0},{9,1},... | collective-permute-start | bytes 1572872 | tf_op jit(solution)/shard_map/ppermute | solution.py:282
  355.2 68.3 %collective-permute-start.23 = (bf16[4,4,8,8,256]{4,3,2,1,0:T(8,128)(2,1)S(1)}, bf16[4,4,8,8,256]{4,3,2,1,0:T(8,128)(2,1)S(1)}, u32[]{:S(2)}, u32[]{:S(2)}) collective-permute-start(bf16[4,4,8,8,256]{4,3,2,1,0:T(8,128)(2,1)S(1)} %copy-done.20), channel_id=1, source_target_pairs={{0,12},{1,13},{2,14},{3,15},{4,8},{5,9},{6,10},{7,11},{8,4},{9,5},... | collective-permute-start | bytes 1572872 | tf_op jit(solution)/shard_map/ppermute | solution.py:282
  361.7 65.3 %collective-permute-start.30 = (bf16[4,4,8,8,256]{4,3,2,1,0:T(8,128)(2,1)S(1)}, bf16[4,4,8,8,256]{4,3,2,1,0:T(8,128)(2,1)S(1)}, u32[]{:S(2)}, u32[]{:S(2)}) collective-permute-start(bf16[4,4,8,8,256]{4,3,2,1,0:T(8,128)(2,1)S(1)} %pad_maximum_fusion.12), channel_id=1, source_target_pairs={{0,4},{1,5},{2,6},{3,7},{4,0},{5,1},{6,2},{7,3},{8,12},{9,13},{10,... | collective-permute-start | bytes 1572872 | tf_op jit(solution)/shard_map/ppermute | solution.py:282
  364.1 77.3 %collective-permute-start.31 = (bf16[4,4,8,8,256]{4,3,2,1,0:T(8,128)(2,1)}, bf16[4,4,8,8,256]{4,3,2,1,0:T(8,128)(2,1)}, u32[]{:S(2)}, u32[]{:S(2)}) collective-permute-start(bf16[4,4,8,8,256]{4,3,2,1,0:T(8,128)(2,1)} %pad_maximum_fusion.13), channel_id=1, source_target_pairs={{0,8},{1,9},{2,10},{3,11},{4,12},{5,13},{6,14},{7,15},{8,0},{9,1},... | collective-permute-start | bytes 1572872 | tf_op jit(solution)/shard_map/ppermute | solution.py:282
  390.7 53.6 %collective-permute-start.32 = (bf16[4,4,8,8,256]{4,3,2,1,0:T(8,128)(2,1)}, bf16[4,4,8,8,256]{4,3,2,1,0:T(8,128)(2,1)}, u32[]{:S(2)}, u32[]{:S(2)}) collective-permute-start(bf16[4,4,8,8,256]{4,3,2,1,0:T(8,128)(2,1)} %pad_maximum_fusion.14), channel_id=1, source_target_pairs={{0,12},{1,13},{2,14},{3,15},{4,8},{5,9},{6,10},{7,11},{8,4},{9,5},... | collective-permute-start | bytes 1572872 | tf_op jit(solution)/shard_map/ppermute | solution.py:282
  424.4 22.7 %collective-permute-start.24 = (bf16[4,4,8,8,256]{4,3,2,1,0:T(8,128)(2,1)}, bf16[4,4,8,8,256]{4,3,2,1,0:T(8,128)(2,1)}, u32[]{:S(2)}, u32[]{:S(2)}) collective-permute-start(bf16[4,4,8,8,256]{4,3,2,1,0:T(8,128)(2,1)} %pad_maximum_fusion.9), channel_id=1, source_target_pairs={{0,1},{1,0},{2,3},{3,2},{4,5},{5,4},{6,7},{7,6},{8,9},{9,8},{10,11... | collective-permute-start | bytes 1572872 | tf_op jit(solution)/shard_map/ppermute | solution.py:282
  425.3 23.6 %collective-permute-start.25 = (bf16[4,4,8,8,256]{4,3,2,1,0:T(8,128)(2,1)}, bf16[4,4,8,8,256]{4,3,2,1,0:T(8,128)(2,1)}, u32[]{:S(2)}, u32[]{:S(2)}) collective-permute-start(bf16[4,4,8,8,256]{4,3,2,1,0:T(8,128)(2,1)} %pad_maximum_fusion.10), channel_id=1, source_target_pairs={{0,2},{1,3},{2,0},{3,1},{4,6},{5,7},{6,4},{7,5},{8,10},{9,11},{10,... | collective-permute-start | bytes 1572872 | tf_op jit(solution)/shard_map/ppermute | solution.py:282
  427.9 21.0 %collective-permute-start.26 = (bf16[4,4,8,8,256]{4,3,2,1,0:T(8,128)(2,1)S(1)}, bf16[4,4,8,8,256]{4,3,2,1,0:T(8,128)(2,1)}, u32[]{:S(2)}, u32[]{:S(2)}) collective-permute-start(bf16[4,4,8,8,256]{4,3,2,1,0:T(8,128)(2,1)S(1)} %pad_maximum_fusion.11), channel_id=1, source_target_pairs={{0,3},{1,2},{2,1},{3,0},{4,7},{5,6},{6,5},{7,4},{8,11},{9,10},{10,... | collective-permute-start | bytes 1572872 | tf_op jit(solution)/shard_map/ppermute | solution.py:282
  441.4 20.1 %collective-permute-start.34 = (bf16[2,2,16,8,512]{4,3,2,1,0:T(8,128)(2,1)S(1)}, bf16[2,2,16,8,512]{4,3,2,1,0:T(8,128)(2,1)S(1)}, u32[]{:S(2)}, u32[]{:S(2)}) collective-permute-start(bf16[2,2,16,8,512]{4,3,2,1,0:T(8,128)(2,1)S(1)} %slice.335), channel_id=1, source_target_pairs={{0,16},{16,0},{1,17},{17,1},{2,18},{18,2},{3,19},{19,3},{4,20},{20... | collective-permute-start | bytes 1572872 | tf_op jit(solution)/shard_map/ppermute | solution.py:291
  444.3 22.9 %collective-permute-start.36 = (bf16[2,2,16,8,512]{4,3,2,1,0:T(8,128)(2,1)S(1)}, bf16[2,2,16,8,512]{4,3,2,1,0:T(8,128)(2,1)S(1)}, u32[]{:S(2)}, u32[]{:S(2)}) collective-permute-start(bf16[2,2,16,8,512]{4,3,2,1,0:T(8,128)(2,1)S(1)} %copy-done.7), channel_id=1, source_target_pairs={{0,8},{1,9},{2,10},{3,11},{4,12},{5,13},{6,14},{7,15},{8,0},{9,1},... | collective-permute-start | bytes 1572872 | tf_op jit(solution)/shard_map/ppermute | solution.py:282
  447.1 22.3 %collective-permute-start.38 = (bf16[16,8,32,128]{3,2,1,0:T(8,128)(2,1)}, bf16[16,8,32,128]{3,2,1,0:T(8,128)(2,1)}, u32[]{:S(2)}, u32[]{:S(2)}) collective-permute-start(bf16[16,8,32,128]{3,2,1,0:T(8,128)(2,1)} %fusion), channel_id=1, source_target_pairs={{0,16},{16,0},{1,17},{17,1},{2,18},{18,2},{3,19},{19,3},{4,20},{20... | collective-permute-start | bytes 3145736 | tf_op jit(solution)/shard_map/ppermute | solution.py:291
  471.9 14.5 %collective-permute-start.41 = (bf16[4,8,32,128]{3,2,1,0:T(8,128)(2,1)S(1)}, bf16[4,8,32,128]{3,2,1,0:T(8,128)(2,1)S(1)}, u32[]{:S(2)}, u32[]{:S(2)}) collective-permute-start(bf16[4,8,32,128]{3,2,1,0:T(8,128)(2,1)S(1)} %get-tuple-element.71), channel_id=1, source_target_pairs={{0,3},{1,2},{2,1},{3,0},{4,7},{5,6},{6,5},{7,4},{8,11},{9,10},{10,... | collective-permute-start | bytes 786440 | tf_op jit(solution)/shard_map/ppermute | solution.py:282
  474.0 13.7 %collective-permute-start.40 = (bf16[4,8,32,128]{3,2,1,0:T(8,128)(2,1)S(1)}, bf16[4,8,32,128]{3,2,1,0:T(8,128)(2,1)S(1)}, u32[]{:S(2)}, u32[]{:S(2)}) collective-permute-start(bf16[4,8,32,128]{3,2,1,0:T(8,128)(2,1)S(1)} %get-tuple-element.72), channel_id=1, source_target_pairs={{0,2},{1,3},{2,0},{3,1},{4,6},{5,7},{6,4},{7,5},{8,10},{9,11},{10,... | collective-permute-start | bytes 786440 | tf_op jit(solution)/shard_map/ppermute | solution.py:282
  (44 other events, 484.5 us)
